TPU v7x, 256 devices: a whole 4x4x8 slice. The times are simulated.
256 devices in a mesh: doc: 64 (over x, z, core), feat: 4 (over y).
Axes of the slice: x: 4, y: 4, z: 8, core: 2. Of those that a mesh axis runs over, the one named last changes fastest.
Arguments:
- b_tiles: bfloat16 [12288, 512, 128], P('doc', 'feat'), may hold values from -0.0625 to 0.0625
- b_rows: int32 [12288, 4], P('doc', 'feat'), may hold values from 0 to 11, as said below
- b_cols: int32 [12288, 4], P('doc', 'feat'), may hold values from 0 to 4095
- b_count: int32 [64, 4], P('doc', 'feat'), may hold values from 144 to 192
- b_offsets: int32 [65], replicated, may hold values from 0 to 480, as said below
- a_tiles: bfloat16 [4096, 512, 128], P('doc', 'feat'), may hold values from -0.375 to 0.375
- a_rows: int32 [4096, 4], P('doc', 'feat'), may hold values from 0 to 12, as said below
- a_tags: int32 [4096, 4], P('doc', 'feat'), may hold values from 0 to 8191, as said below
- a_count: int32 [64, 4], P('doc', 'feat'), may hold values from 48 to 64
- a_offsets: int32 [65], replicated, may hold values from 0 to 480, as said below
- omega_seed: int32 [1], replicated, may hold values from 0 to 1073741823
Outputs:
- tag_sketch: float32 [1048576, 256], P(('doc', 'feat'))
Inputs may be any that keep to these rules, and one draw needn't show every extreme that they name: b_offsets[0] is 0 and each device's range of the text view holds 3 to 12 row blocks. a_offsets[0] is 0 and a_offsets[64] equals b_offsets[64]; every other entry lies 1 to 2 row blocks below the same entry of b_offsets; each device's range of the tag view holds at most 13 row blocks. `b_rows`: below the number of row blocks of the device's range of the text view. `a_rows`: below the number of row blocks of the device's range of the tag view. `a_tags`: the rows of a tile's tag block lie, under the output's placement, on a device with the same feat index as the tile; on one device at most 2 tiles in use have tag blocks on devices of one doc index, and in every draw some doc index gets exactly 2 tiles in use from every device.
All inputs are finite; a program needn't handle non-finite values.
Results may differ from a plain program's by a relative error of at most 0.004.
Values may be sent and summed in bfloat16 or wider, within the bound.
A program may use at most 128 MiB of HBM per device.

v0:
```python
import jax
import jax.numpy as jnp
from jax import lax
from jax.sharding import PartitionSpec as P

TILE = 128
SKETCH = 256
TERMS = 2097152
TAG_DEV = 4096
ROWB_MAX = 12
MARGIN = 2
ROWA_MAX = 13


def passed_along(block, axis, distance):
    devices = range(lax.axis_size(axis))
    route = [(i - distance, i) for i in devices if i - distance in devices]
    return lax.ppermute(block, axis, route)


def unsigned_shift(value, count):
    return lax.shift_right_logical(value, jnp.full(value.shape, count, jnp.int32))


def omega_panel(term_blocks, seed_value):
    row_iota = lax.broadcasted_iota(jnp.int32, (1, TILE, SKETCH), 1)
    col_iota = lax.broadcasted_iota(jnp.int32, (1, TILE, SKETCH), 2)
    mixing = (term_blocks[:, None, None] * TILE + row_iota) * SKETCH + col_iota
    mixing = mixing ^ seed_value * 747796405
    mixing = mixing ^ unsigned_shift(mixing, 16)
    mixing = mixing * 2146121005
    mixing = mixing ^ unsigned_shift(mixing, 15)
    mixing = mixing * -2073254261
    mixing = mixing ^ unsigned_shift(mixing, 16)
    levels = (unsigned_shift(mixing, 8) & 65535).astype(jnp.float32)
    return ((levels - 32767.5) * (3.4641016 / 65536.0)).astype(jnp.bfloat16)


def local(
    b_tiles,
    b_rows,
    b_cols,
    b_count,
    b_offsets,
    a_tiles,
    a_rows,
    a_tags,
    a_count,
    a_offsets,
    omega_seed,
):
    doc_count = lax.axis_size("doc")
    feat_count = lax.axis_size("feat")
    doc_here = lax.axis_index("doc")
    feat_here = lax.axis_index("feat")
    tiles_b = b_tiles.shape[0]
    tiles_a = a_tiles.shape[0]
    highest = lax.Precision.HIGHEST
    slab_blocks = TERMS // (TILE * feat_count)
    panels = omega_panel(b_cols[:, 0] + feat_here * slab_blocks, omega_seed[0])
    tile_terms = jnp.einsum("tij,tjk->tik", b_tiles, panels, preferred_element_type=jnp.float32)
    live_b = jnp.arange(tiles_b, dtype=jnp.int32) < b_count[0, 0]
    chosen = (b_rows[:, 0][None, :] == jnp.arange(ROWB_MAX, dtype=jnp.int32)[:, None]) & live_b[
        None, :
    ]
    partial_value = jnp.einsum(
        "rt,tik->rik", chosen.astype(jnp.float32), tile_terms, precision=highest
    )
    b_start = b_offsets[doc_here]
    b_length = b_offsets[doc_here + 1] - b_start
    shift_rows = a_offsets[doc_here] - b_start + MARGIN
    own_rows = lax.psum(partial_value, "feat").astype(jnp.bfloat16)
    last_rows = lax.dynamic_slice_in_dim(own_rows, b_length - MARGIN, MARGIN, 0)
    arrived = passed_along(last_rows, "doc", 1)
    source = jnp.concatenate([arrived, own_rows], axis=0)
    row_picks = jnp.clip(
        jnp.arange(ROWA_MAX, dtype=jnp.int32) + shift_rows, 0, MARGIN + ROWB_MAX - 1
    )
    z_rows = jnp.take(source, row_picks, axis=0)
    live_a = jnp.arange(tiles_a, dtype=jnp.int32) < a_count[0, 0]
    tile_rows = jnp.take(z_rows, a_rows[:, 0], axis=0)
    tag_blocks = a_tags[:, 0]
    owned_blocks = TAG_DEV // TILE
    capacity = max(2, (tiles_a + doc_count - 1) // doc_count)
    owner_doc = tag_blocks // owned_blocks // feat_count
    owner_hits = (
        (owner_doc[:, None] == jnp.arange(doc_count, dtype=jnp.int32)[None, :]) & live_a[:, None]
    ).astype(jnp.int32)
    earlier = jnp.cumsum(owner_hits, axis=0) - owner_hits
    ranking = jnp.sum(earlier * owner_hits, axis=1)
    slot_index = jnp.where(live_a, owner_doc * capacity + ranking, doc_count * capacity)
    sent_ids = (
        jnp.full((doc_count * capacity,), -1, jnp.int32)
        .at[slot_index]
        .set(tag_blocks, mode="drop")
        .reshape(doc_count, capacity)
    )
    products = jnp.einsum("tij,tik->tjk", a_tiles, tile_rows, preferred_element_type=jnp.float32)
    outbox = (
        jnp.zeros((doc_count * capacity, TILE, SKETCH), jnp.float32)
        .at[slot_index]
        .set(products, mode="drop")
    )
    arrived_sums, arrived_ids = (
        lax.all_to_all(
            outbox.reshape(doc_count, capacity, TILE, SKETCH),
            "doc",
            split_axis=0,
            concat_axis=0,
            tiled=True,
        ),
        lax.all_to_all(sent_ids, "doc", split_axis=0, concat_axis=0, tiled=True),
    )
    flat_here = doc_here * feat_count + feat_here
    local_blocks = arrived_ids.reshape(-1) - flat_here * owned_blocks
    block_pick = (
        jnp.arange(owned_blocks, dtype=jnp.int32)[:, None] == local_blocks[None, :]
    ).astype(jnp.float32)
    sketch = jnp.einsum(
        "bs,sjk->bjk", block_pick, arrived_sums.reshape(-1, TILE, SKETCH), precision=highest
    )
    return sketch.reshape(TAG_DEV, SKETCH)


def solution(mesh):
    return jax.shard_map(
        local,
        mesh=mesh,
        in_specs=(
            P("doc", "feat", None),
            P("doc", "feat"),
            P("doc", "feat"),
            P("doc", "feat"),
            P(),
            P("doc", "feat", None),
            P("doc", "feat"),
            P("doc", "feat"),
            P("doc", "feat"),
            P(),
            P(),
        ),
        out_specs=P(("doc", "feat"), None),
        check_vma=False,
    )
```

profile of v0, /device:TPU:24, one launch (start us, length us, event | category | flops | bytes accessed | tf_op | source)
XLA Modules:
  0.0 619.5 jit_solution(13340459511408527445)
XLA Ops:
  0.0 1.4 fusion.58
  3.3 0.7 add_multiply_fusion
  4.0 18.3 %fusion.21 = f32[192,128,256]{1,2,0:T(8,128)} fusion(bf16[192,128,128]{2,1,0:T(8,128)(2,1)} %param.11, s32[]{:T(128)} %bitcast.13, s32[192]{0:T(256)S(1)} %bitcast.49), kind=kOutput, calls=%fused_computation.27 | convolution fusion | flops 1723858944 | bytes 31458052 | tf_op jit(solution)/shard_map/tij,tjk->tik/dot_general | solution.py:61
  22.3 24.8 %copy.21 = f32[192,128,256]{2,0,1:T(8,128)} copy(f32[192,128,256]{1,2,0:T(8,128)} %fusion.21) | data formatting | bytes 50331648 | tf_op jit(solution)/shard_map/tij,tjk->tik/dot_general | solution.py:61
  47.9 13.5 %fusion.38 = f32[12,128,256]{2,0,1:T(8,128)} fusion(f32[192,128,256]{2,0,1:T(8,128)} %copy.21, s32[192]{0:T(256)S(1)} %bitcast.48, pred[192]{0:T(512)(128)(4,1)S(1)} %iota_compare_fusion.3), kind=kOutput, calls=%fused_computation.46 | convolution fusion | flops 905974272 | bytes 26739648 | tf_op jit(solution)/shard_map/rt,tik->rik/dot_general | solution.py:66
  61.4 42.4 %all-reduce.1 = bf16[12,128,256]{2,0,1:T(8,128)(2,1)S(1)} all-reduce(f32[12,128,256]{2,0,1:T(8,128)} %fusion.38), channel_id=1, replica_groups=mesh['doc'=64,'feat'=4] {'feat'}, use_global_device_ids=true, to_apply=%region_3.4 | all-reduce | flops 393216 | bytes 2359296 | tf_op jit(solution)/shard_map/psum | solution.py:72
  104.0 1.3 collective-permute-start
  106.4 0.8 scatter_custom_fusion
  107.2 0.7 all_to_all.9
  107.9 13.5 %all-to-all-start = ((s32[64,1,2]{2,1,0:T(1,128)}), s32[64,1,2]{2,1,0:T(1,128)S(1)}, u32[]{:S(2)}, u32[]{:S(2)}) async-start(s32[64,1,2]{2,1,0:T(1,128)} %bitcast.5), calls=%async_computation | async-start | bytes 65536 | tf_op jit(solution)/shard_map/all_to_all | solution.py:112
  124.2 1.5 gather_fusion
  125.7 1.3 broadcast_select_fusion
  127.0 2.8 gather_fusion.1
  129.8 6.8 %fusion.27 = f32[64,128,256]{1,2,0:T(8,128)} fusion(bf16[64,128,128]{2,1,0:T(8,128)(2,1)S(1)} %copy-done, bf16[64,128,256]{2,1,0:T(8,128)(2,1)} %gather_fusion.1, pred[64]{0:T(512)(128)(4,1)S(1)} %and_bitcast_fusion), kind=kOutput, calls=%fused_computation.31 | convolution fusion | flops 538968064 | bytes 14680128 | tf_op jit(solution)/shard_map/tij,tik->tjk/dot_general | solution.py:98
  136.6 9.0 %copy.24 = f32[64,128,256]{2,1,0:T(8,128)} copy(f32[64,128,256]{1,2,0:T(8,128)} %fusion.27) | data formatting | bytes 16777216 | tf_op jit(solution)/shard_map/tij,tik->tjk/dot_general | solution.py:98
  145.6 7.8 %broadcast_in_dim.48 = f32[128,128,256]{2,1,0:T(8,128)} broadcast(f32[]{:T(128)} %constant.99.clone.1), dimensions={} | broadcast | bytes 16777220 | tf_op jit(solution)/shard_map/broadcast_in_dim | solution.py:100
  153.4 16.0 %scatter_fusion = f32[128,128,256]{2,1,0:T(8,128)} fusion(f32[128,128,256]{2,1,0:T(8,128)} %broadcast_in_dim.48, s32[64]{0:T(128)S(1)} %fusion.44, f32[64,128,256]{2,1,0:T(8,128)} %copy.24), kind=kCustom, calls=%fused_computation.3 | custom fusion | bytes 25166080 | tf_op jit(solution)/shard_map/scatter | solution.py:102
  169.4 28.5 %copy.25 = f32[64,2,128,256]{3,1,2,0:T(2,128)} copy(f32[64,2,128,256]{3,2,1,0:T(8,128)} %bitcast.47) | data formatting | bytes 33554432 | tf_op jit(solution)/shard_map/reshape | solution.py:106
  197.9 10.6 %all-to-all-start.1 = ((f32[64,2,128,256]{3,1,2,0:T(2,128)}), f32[64,2,128,256]{3,1,2,0:T(2,128)}, u32[]{:S(2)}, u32[]{:S(2)}) async-start(f32[64,2,128,256]{3,1,2,0:T(2,128)} %copy.25), calls=%async_computation.1 | async-start | bytes 33554432 | tf_op jit(solution)/shard_map/all_to_all | solution.py:105
  208.7 364.2 %all-to-all-done.1 = f32[64,2,128,256]{3,1,2,0:T(2,128)} async-done(((f32[64,2,128,256]{3,1,2,0:T(2,128)}), f32[64,2,128,256]{3,1,2,0:T(2,128)}, u32[]{:S(2)}, u32[]{:S(2)}) %all-to-all-start.1) | async-done | bytes 16777248 | tf_op jit(solution)/shard_map/all_to_all | solution.py:105
  572.9 12.1 %copy.26 = f32[64,2,128,256]{3,1,0,2:T(2,128)} copy(f32[64,2,128,256]{3,1,2,0:T(2,128)} %all-to-all-done.1) | data formatting | bytes 33554432 | tf_op jit(solution)/shard_map/all_to_all | solution.py:105
  585.0 20.7 %reshape.87 = f32[128,128,256]{2,0,1:T(8,128)} reshape(f32[64,2,128,256]{3,1,0,2:T(2,128)} %copy.26) | data formatting | bytes 33554432 | tf_op jit(solution)/shard_map/reshape | solution.py:120
  605.7 9.4 %fusion.34 = f32[32,128,256]{2,0,1:T(8,128)S(1)} fusion(f32[128,128,256]{2,0,1:T(8,128)} %reshape.87, s32[128]{0:T(128)S(1)} %sub.48), kind=kOutput, calls=%fused_computation.43 | convolution fusion | flops 1610616832 | bytes 20972032 | tf_op jit(solution)/shard_map/bs,sjk->bjk/dot_general | solution.py:119
  615.1 4.4 copy.27
  (33 shorter events, 2.3 us)
Async XLA Ops:
  0.0 129.8 %copy-start = (bf16[64,128,128]{2,1,0:T(8,128)(2,1)S(1)}, bf16[64,128,128]{2,1,0:T(8,128)(2,1)}, u32[]{:S(2)}) copy-start(bf16[64,128,128]{2,1,0:T(8,128)(2,1)} %param.16) | copy-start | bytes 6291460
  22.3 25.6 %copy-start.2 = (s32[192,1]{0,1:T(1,128)S(1)}, s32[192,1]{0,1:T(1,128)}, u32[]{:S(2)}) copy-start(s32[192,1]{0,1:T(1,128)} %param.12) | copy-start | bytes 2308
  47.2 58.8 %copy-start.3 = (s32[64,1]{0,1:T(1,128)S(1)}, s32[64,1]{0,1:T(1,128)}, u32[]{:S(2)}) copy-start(s32[64,1]{0,1:T(1,128)} %param.18) | copy-start | bytes 772
  47.2 74.2 %copy-start.4 = (s32[64,1]{0,1:T(1,128)S(1)}, s32[64,1]{0,1:T(1,128)}, u32[]{:S(2)}) copy-start(s32[64,1]{0,1:T(1,128)} %param.17) | copy-start | bytes 772
  47.2 74.2 %copy-start.5 = (s32[65]{0:T(128)S(1)}, s32[65]{0:T(128)}, u32[]{:S(2)}) copy-start(s32[65]{0:T(128)} %param.20) | copy-start | bytes 784
  104.0 19.3 %collective-permute-start = (bf16[2,128,256]{2,0,1:T(2,128)(2,1)S(1)}, bf16[2,128,256]{2,0,1:T(2,128)(2,1)S(1)}, u32[]{:S(2)}, u32[]{:S(2)}) collective-permute-start(bf16[2,128,256]{2,0,1:T(2,128)(2,1)S(1)} %constant_dynamic-slice_fusion), channel_id=1, source_target_pairs={{0,4},{4,8},{8,12},{12,16},{16,20},{20,24},{24,28},{28,32},{32,36}... | collective-permute-start | bytes 393224 | tf_op jit(solution)/shard_map/ppermute | solution.py:18
  107.9 90.0 %all-to-all-start = ((s32[64,1,2]{2,1,0:T(1,128)}), s32[64,1,2]{2,1,0:T(1,128)S(1)}, u32[]{:S(2)}, u32[]{:S(2)}) async-start(s32[64,1,2]{2,1,0:T(1,128)} %bitcast.5), calls=%async_computation | async-start | bytes 65536 | tf_op jit(solution)/shard_map/all_to_all | solution.py:112
  197.9 375.0 %all-to-all-start.1 = ((f32[64,2,128,256]{3,1,2,0:T(2,128)}), f32[64,2,128,256]{3,1,2,0:T(2,128)}, u32[]{:S(2)}, u32[]{:S(2)}) async-start(f32[64,2,128,256]{3,1,2,0:T(2,128)} %copy.25), calls=%async_computation.1 | async-start | bytes 33554432 | tf_op jit(solution)/shard_map/all_to_all | solution.py:105
  585.0 34.5 %copy-start.1 = (bf16[64,128,128]{2,1,0:T(8,128)(2,1)S(1)}, bf16[64,128,128]{2,1,0:T(8,128)(2,1)}, u32[]{:S(2)}) copy-start(bf16[64,128,128]{2,1,0:T(8,128)(2,1)} %param.16) | copy-start | bytes 6291460
where the time goes:
time: 624 us; the launch traced here: 620 us
  waiting for transfers between devices  364 us (58%)
  local copies, waits for them, and re-layouts  132 us (21%)
  matrix products  48 us (8%)
  blocking collectives  42.4 us (7%)
  starting transfers between devices  25.3 us (4%)
    all_to_all x1, waiting for transfers between devices, local(): lax.all_to_all(outbox.reshape(doc_count, capacity, TILE, SKETCH), 'doc',...  364 us
    psum x1, blocking collectives, local(): own_rows = lax.psum(partial_value, 'feat').astype(jnp.bfloat16)  42.4 us
    reshape x1, local copies, waits for them, and re-layouts, local(): outbox.reshape(doc_count, capacity, TILE, SKETCH)  28.5 us
    dot_general x1, local copies, waits for them, and re-layouts, local(): jnp.einsum('tij,tjk->tik', b_tiles, panels, preferred_element_type=jnp.fl...  24.8 us
    reshape x1, local copies, waits for them, and re-layouts, local(): arrived_sums.reshape(-1, TILE, SKETCH)  20.7 us
    dot_general x1, matrix products, local(): jnp.einsum('tij,tjk->tik', b_tiles, panels, preferred_element_type=jnp.fl...  18.3 us
    scatter x1, local copies, waits for them, and re-layouts, local(): outbox = jnp.zeros((doc_count * capacity, TILE, SKETCH), jnp.float32).at[...  16 us
    dot_general x1, matrix products, local(): jnp.einsum('rt,tik->rik', chosen.astype(jnp.float32), tile_terms, precisi...  13.5 us
  transfers between devices with their start and end apart: 3, of which 1 were waited for; matrix products, arithmetic and copies ran while one was open for 12% of the time, Pallas kernels for 0%

commit v1 on v0

v1 whole, which is shorter than its diff:
```python
import functools

import jax
import jax.numpy as jnp
from jax import lax
from jax.experimental import pallas as pl
from jax.experimental.pallas import tpu as pltpu
from jax.sharding import PartitionSpec as P

TILE = 128
SKETCH = 256
TERMS = 2097152
TAG_DEV = 4096
ROWB_MAX = 12
OWNED = TAG_DEV // TILE
N_DOC = 64
N_FEAT = 4
META = 16
PAGE = 2 * TILE + META
CHUNK = 16
GROUP = 4
DEPTH = 8

VMEM = pltpu.MemorySpace.VMEM
SMEM = pltpu.MemorySpace.SMEM
ANY = pl.ANY


def shr(value, count):
    return lax.shift_right_logical(value, jnp.full(value.shape, count, jnp.int32))


def text_kernel(rows, cols, count, seed, tiles, out, acc, base):
    step = pl.program_id(0)

    @pl.when(step == 0)
    def _():
        row_iota = lax.broadcasted_iota(jnp.int32, (TILE, SKETCH), 0)
        col_iota = lax.broadcasted_iota(jnp.int32, (TILE, SKETCH), 1)
        start = (row_iota * SKETCH + col_iota) ^ (seed[0] * 747796405)
        base[...] = start ^ shr(start, 16)
        acc[...] = jnp.zeros_like(acc)

    slab = lax.axis_index("feat") * (TERMS // (TILE * N_FEAT))
    used = count[0]

    def some(group, carry):
        products = []
        for lane in range(GROUP):
            at = group * GROUP + lane
            block = (cols[step * CHUNK + at] + slab) * (TILE * SKETCH)
            block = block ^ lax.shift_right_logical(block, jnp.int32(16))
            mixing = base[...] ^ block
            mixing = mixing * 2146121005
            mixing = mixing ^ shr(mixing, 15)
            mixing = mixing * -2073254261
            mixing = mixing ^ shr(mixing, 16)
            levels = (shr(mixing, 8) & 65535).astype(jnp.float32)
            panel = ((levels - 32767.5) * (3.4641016 / 65536.0)).astype(jnp.bfloat16)
            products.append(jnp.dot(tiles[at], panel, preferred_element_type=jnp.float32))
        for lane in range(GROUP):
            at = step * CHUNK + group * GROUP + lane
            place = jnp.where(at < used, rows[at], ROWB_MAX)
            acc[place] += products[lane]
        return carry

    left = jnp.clip(used - step * CHUNK, 0, CHUNK)
    lax.fori_loop(0, (left + GROUP - 1) // GROUP, some, 0)

    @pl.when(step == pl.num_programs(0) - 1)
    def _():
        out[...] = acc[0:ROWB_MAX]


def text_stage(b_rows, b_cols, b_count, omega_seed, b_tiles):
    tiles_b = b_tiles.shape[0]
    return pl.pallas_call(
        text_kernel,
        out_shape=jax.ShapeDtypeStruct((ROWB_MAX, TILE, SKETCH), jnp.float32),
        grid=(tiles_b // CHUNK,),
        in_specs=[
            pl.BlockSpec(memory_space=SMEM),
            pl.BlockSpec(memory_space=SMEM),
            pl.BlockSpec(memory_space=SMEM),
            pl.BlockSpec(memory_space=SMEM),
            pl.BlockSpec((CHUNK, TILE, TILE), lambda i: (i, 0, 0)),
        ],
        out_specs=pl.BlockSpec((ROWB_MAX, TILE, SKETCH), lambda i: (0, 0, 0)),
        scratch_shapes=[
            pltpu.VMEM((ROWB_MAX + 1, TILE, SKETCH), jnp.float32),
            pltpu.VMEM((TILE, SKETCH), jnp.int32),
        ],
        cost_estimate=pl.CostEstimate(flops=1700000000, bytes_accessed=8000000, transcendentals=0),
    )(b_rows, b_cols, b_count, omega_seed, b_tiles)


def pack_kernel(tags, rows, count, tiles, outbox, meta, seen, notes, sems, meta_sem):
    used = count[0]

    def clear(owner, carry):
        seen[owner] = 0
        for lane in range(4):
            notes[owner * 4 + lane] = 0
        return carry

    lax.fori_loop(0, N_DOC, clear, 0)

    def copy(at, owner, rank):
        start = pl.multiple_of(rank * TILE, TILE)
        return pltpu.make_async_copy(
            tiles.at[at], outbox.at[owner, pl.ds(start, TILE), :], sems.at[at]
        )

    def send(at, carry):
        tag = tags[at]
        owner = lax.shift_right_logical(tag, jnp.int32(7))
        rank = jnp.minimum(seen[owner], 1)
        seen[owner] = rank + 1
        notes[owner * 4 + rank * 2] = (tag & (OWNED - 1)) + 1
        notes[owner * 4 + rank * 2 + 1] = rows[at]
        copy(at, owner, rank).start()
        return carry

    lax.fori_loop(0, used, send, 0)
    lane_iota = lax.broadcasted_iota(jnp.int32, (META, TILE), 1)

    def note(owner, carry):
        value = jnp.zeros((META, TILE), jnp.int32)
        for lane in range(4):
            value = jnp.where(lane_iota == lane, notes[owner * 4 + lane], value)
        meta[owner] = value.astype(jnp.float32).astype(jnp.bfloat16)
        return carry

    lax.fori_loop(0, N_DOC, note, 0)
    last = pltpu.make_async_copy(meta, outbox.at[:, pl.ds(2 * TILE, META), :], meta_sem)
    last.start()

    def drain(at, carry):
        copy(at, 0, 0).wait()
        return carry

    lax.fori_loop(0, used, drain, 0)
    last.wait()


def pack_stage(a_tags, a_rows, a_count, a_tiles):
    tiles_a = a_tiles.shape[0]
    return pl.pallas_call(
        pack_kernel,
        out_shape=jax.ShapeDtypeStruct((N_DOC, PAGE, TILE), jnp.bfloat16),
        in_specs=[
            pl.BlockSpec(memory_space=SMEM),
            pl.BlockSpec(memory_space=SMEM),
            pl.BlockSpec(memory_space=SMEM),
            pl.BlockSpec(memory_space=VMEM),
        ],
        out_specs=pl.BlockSpec(memory_space=ANY),
        scratch_shapes=[
            pltpu.VMEM((N_DOC, META, TILE), jnp.bfloat16),
            pltpu.SMEM((N_DOC,), jnp.int32),
            pltpu.SMEM((N_DOC * 4,), jnp.int32),
            pltpu.SemaphoreType.DMA((tiles_a,)),
            pltpu.SemaphoreType.DMA,
        ],
    )(a_tags, a_rows, a_count, a_tiles)


def final_kernel(notes, b_offsets, a_offsets, inbox, gathered, out, lists, zbuf, sems):
    def listed(doc, found):
        shift = a_offsets[doc] - b_offsets[doc]
        before = b_offsets[doc] - b_offsets[jnp.maximum(doc - 1, 0)]
        for rank in range(2):
            tag = notes[doc * 4 + rank * 2] - 1
            row = notes[doc * 4 + rank * 2 + 1] + shift
            index = jnp.where(
                row < 0, (doc - 1) * ROWB_MAX + row + before, doc * ROWB_MAX + row
            )
            lists[0, found] = tag
            lists[1, found] = jnp.maximum(index, 0)
            lists[2, found] = doc * 2 + rank
            found = found + (tag >= 0).astype(jnp.int32)
        return found

    total = lax.fori_loop(0, N_DOC, listed, 0)

    def fetch(at, slot):
        return pltpu.make_async_copy(gathered.at[lists[1, at]], zbuf.at[slot], sems.at[slot])

    for first in range(DEPTH):

        @pl.when(first < total)
        def _():
            fetch(first, first).start()

    out[...] = jnp.zeros_like(out)

    def add(at, carry):
        slot = lax.rem(at, DEPTH)
        fetch(at, slot).wait()
        source = lists[2, at]
        start = pl.multiple_of((source & 1) * TILE, TILE)
        tile = inbox[lax.shift_right_logical(source, jnp.int32(1)), pl.ds(start, TILE), :]
        product = lax.dot_general(
            tile, zbuf[slot], (((0,), (0,)), ((), ())), preferred_element_type=jnp.float32
        )
        place = pl.multiple_of(lists[0, at] * TILE, TILE)
        out[pl.ds(place, TILE), :] += product

        @pl.when(at + DEPTH < total)
        def _():
            fetch(at + DEPTH, slot).start()

        return carry

    lax.fori_loop(0, total, add, 0)


def final_stage(notes, b_offsets, a_offsets, inbox, gathered):
    return pl.pallas_call(
        final_kernel,
        out_shape=jax.ShapeDtypeStruct((TAG_DEV, SKETCH), jnp.float32),
        in_specs=[
            pl.BlockSpec(memory_space=SMEM),
            pl.BlockSpec(memory_space=SMEM),
            pl.BlockSpec(memory_space=SMEM),
            pl.BlockSpec(memory_space=VMEM),
            pl.BlockSpec(memory_space=ANY),
        ],
        out_specs=pl.BlockSpec(memory_space=VMEM),
        scratch_shapes=[
            pltpu.SMEM((3, 2 * N_DOC + 1), jnp.int32),
            pltpu.VMEM((DEPTH, TILE, SKETCH), jnp.bfloat16),
            pltpu.SemaphoreType.DMA((DEPTH,)),
        ],
    )(notes, b_offsets, a_offsets, inbox, gathered)


def local(
    b_tiles,
    b_rows,
    b_cols,
    b_count,
    b_offsets,
    a_tiles,
    a_rows,
    a_tags,
    a_count,
    a_offsets,
    omega_seed,
):
    outbox = pack_stage(a_tags[:, 0], a_rows[:, 0], a_count[:, 0], a_tiles)
    inbox = lax.all_to_all(outbox, "doc", split_axis=0, concat_axis=0, tiled=True)
    partial = text_stage(b_rows[:, 0], b_cols[:, 0], b_count[:, 0], omega_seed, b_tiles)
    mine = lax.psum_scatter(partial, "feat", scatter_dimension=0, tiled=True)
    gathered = lax.all_gather(mine.astype(jnp.bfloat16), ("doc", "feat"))
    notes = inbox[:, 2 * TILE, 0:4].astype(jnp.int32).reshape(-1)
    return final_stage(
        notes,
        b_offsets,
        a_offsets,
        inbox,
        gathered.reshape(N_DOC * ROWB_MAX, TILE, SKETCH),
    )


def solution(mesh):
    return jax.shard_map(
        local,
        mesh=mesh,
        in_specs=(
            P("doc", "feat", None),
            P("doc", "feat"),
            P("doc", "feat"),
            P("doc", "feat"),
            P(),
            P("doc", "feat", None),
            P("doc", "feat"),
            P("doc", "feat"),
            P("doc", "feat"),
            P(),
            P(),
        ),
        out_specs=P(("doc", "feat"), None),
        check_vma=False,
    )
```

time: 624 us -> 333 us (0.53)
  waiting for transfers between devices: 364 us -> 122 us
  local copies, waits for them, and re-layouts: 132 us -> 2.76 us
  blocking collectives: 42.4 us -> 137 us
  Pallas kernels: 0 us -> 49.4 us
  matrix products: 48 us -> 0 us
  starting transfers between devices: 25.3 us -> 0.04 us
  between operations: 4.73 us -> 15.4 us
    all_to_all x2 -> x0, waiting for transfers between devices: 364 us -> none  [the longest x1 364 us: local(): lax.all_to_all(outbox.reshape(doc_count, capacity, TILE, SKETCH), 'doc',...]
    all_to_all x0 -> x1, blocking collectives: none -> 137 us  [local(): lax.all_to_all(outbox, 'doc', split_axis=0, concat_axis=0, tiled=True)]
    all_gather x0 -> x1, waiting for transfers between devices: none -> 90.9 us  [local(): gathered = lax.all_gather(mine.astype(jnp.bfloat16), ('doc', 'feat'))]
    pallas_call x0 -> x3, Pallas kernels: none -> 49.4 us  [the longest x1 25.2 us: final_stage(): pl.pallas_call(final_kernel, out_shape=jax.ShapeDtypeStruct((TAG_DEV, SKE...]
    reshape x2 -> x0, local copies, waits for them, and re-layouts: 49.2 us -> none  [the longest x1 28.5 us: local(): outbox.reshape(doc_count, capacity, TILE, SKETCH)]
    dot_general x4 -> x0, matrix products: 48 us -> none  [the longest x1 18.3 us: local(): jnp.einsum('tij,tjk->tik', b_tiles, panels, preferred_element_type=jnp.fl...]
    psum x1 -> x0, blocking collectives: 42.4 us -> none  [local(): own_rows = lax.psum(partial_value, 'feat').astype(jnp.bfloat16)]
    dot_general x3 -> x0, local copies, waits for them, and re-layouts: 38.3 us -> none  [the longest x1 24.8 us: local(): jnp.einsum('tij,tjk->tik', b_tiles, panels, preferred_element_type=jnp.fl...]
  transfers between devices with their start and end apart: 3 -> 2, of which waited for: 1 -> 2; matrix products, arithmetic and copies ran while one was open for 12% -> 0% of each run, Pallas kernels for 0% -> 1%
where the time goes in v1:
time: 333 us; the launch traced here: 328 us
  blocking collectives  137 us (41%)
  waiting for transfers between devices  122 us (37%)
  Pallas kernels  49.4 us (15%)
  between operations  15.4 us (5%)
    all_to_all x1, blocking collectives, local(): lax.all_to_all(outbox, 'doc', split_axis=0, concat_axis=0, tiled=True)  137 us
    all_gather x1, waiting for transfers between devices, local(): gathered = lax.all_gather(mine.astype(jnp.bfloat16), ('doc', 'feat'))  90.9 us
    reduce_scatter x1, waiting for transfers between devices, local(): mine = lax.psum_scatter(partial, 'feat', scatter_dimension=0, tiled=True)  31.3 us
    pallas_call x1, Pallas kernels, final_stage(): pl.pallas_call(final_kernel, out_shape=jax.ShapeDtypeStruct((TAG_DEV, SKE...  25.2 us
    pallas_call x1, Pallas kernels, text_stage(): pl.pallas_call(text_kernel, out_shape=jax.ShapeDtypeStruct((ROWB_MAX, TIL...  19.3 us
  transfers between devices with their start and end apart: 2, of which 2 were waited for; matrix products, arithmetic and copies ran while one was open for 0% of the time, Pallas kernels for 1%

profile of v1, /device:TPU:24, one launch (start us, length us, event | category | flops | bytes accessed | tf_op | source)
XLA Modules:
  0.0 328.3 jit_solution(4192655863253889183)
XLA Ops:
  6.5 0.0 reduce-scatter.2.cloned.1.call-start
  7.8 19.3 %shard_map.110 = f32[12,128,256]{2,1,0:T(8,128)} custom-call(s32[192]{0:T(256)} %bitcast.8, s32[192]{0:T(256)} %bitcast.9, s32[1]{0:T(128)} %bitcast.6.count, s32[1]{0:T(128)S(6)} %copy.14.seed, bf16[192,128,128]{2,1,0:T(8,128)(2,1)} %tiles.3), custom_call_target="tpu_custom_call" | custom-call | flops 1700000000 | bytes 8000000 | tf_op jit(solution)/shard_map/pallas_call | solution.py:77
  27.2 0.0 reduce-scatter.2.cloned.1.call-update
  27.2 0.0 all-gather.3.cloned.1.call-start
  27.2 31.3 %reduce-scatter.2.cloned.1.call-done = f32[3,128,256]{2,1,0:T(8,128)} async-done(((f32[12,128,256]{2,1,0:T(8,128)}), f32[3,128,256]{2,1,0:T(8,128)}) %reduce-scatter.2.cloned.1.call-update) | async-done | bytes 393232 | tf_op jit(solution)/shard_map/reduce_scatter | solution.py:254
  58.5 1.7 convert_element_type.12
  60.2 0.0 all-gather.3.cloned.1.call-update
  60.9 4.9 %shard_map.109 = bf16[64,272,128]{2,1,0:T(8,128)(2,1)} custom-call(s32[64]{0:T(128)} %bitcast.10, s32[64]{0:T(128)} %bitcast.11, s32[1]{0:T(128)} %bitcast.7.count, bf16[64,128,128]{2,1,0:T(8,128)(2,1)} %tiles.2), custom_call_target="tpu_custom_call" | custom-call | tf_op jit(solution)/shard_map/pallas_call | solution.py:148
  65.7 136.8 %all_to_all.5.inbox = bf16[64,272,128]{2,1,0:T(8,128)(2,1)S(1)} all-to-all(bf16[64,272,128]{2,1,0:T(8,128)(2,1)} %shard_map.109), channel_id=1, replica_groups=mesh['doc'=64,'feat'=4] {'doc'}, dimensions={0} | all-to-all | bytes 8912896 | tf_op jit(solution)/shard_map/all_to_all | solution.py:252
  202.6 0.0 copy-start
  202.6 2.1 copy-done
  204.7 0.1 fusion
  204.8 0.6 reshape.8.notes
  205.4 90.9 %all-gather.3.cloned.1.call-done.gathered = bf16[768,128,256]{2,1,0:T(8,128)(2,1)} async-done(((bf16[3,128,256]{2,1,0:T(8,128)(2,1)}), bf16[768,128,256]{2,1,0:T(8,128)(2,1)}) %all-gather.3.cloned.1.call-update) | async-done | bytes 50331664 | tf_op jit(solution)/shard_map/all_gather | solution.py:255
  296.3 25.2 %shard_map.111 = f32[4096,256]{1,0:T(8,128)} custom-call(s32[256]{0:T(256)} %reshape.8.notes, s32[65]{0:T(128)} %b_offsets.1, s32[65]{0:T(128)} %a_offsets.1, bf16[64,272,128]{2,1,0:T(8,128)(2,1)} %copy-done, bf16[768,128,256]{2,1,0:T(8,128)(2,1)} %all-gather.3.cloned.1.call-done.gathered), custom_call_target="tpu_custom_call" | custom-call | tf_op jit(solution)/shard_map/pallas_call | solution.py:219
Async XLA Ops:
  6.5 52.0 %reduce-scatter.2.cloned.1.call-start = ((), (), s32[]{:S(2)}) async-start(), calls=%async_computation.2 | async-start | bytes 1966080 | tf_op jit(solution)/shard_map/reduce_scatter | solution.py:254
  27.2 269.1 %all-gather.3.cloned.1.call-start = ((), (), s32[]{:S(2)}) async-start(), calls=%async_computation.3 | async-start | bytes 50528256 | tf_op jit(solution)/shard_map/all_gather | solution.py:255
  202.6 2.1 copy-start
Sparse Core Ops, SparseCore 0:
  27.3 31.1 reduce-scatter.1
  62.3 233.9 all-gather.2

commit v2 on v1

--- a/solution.py
+++ b/solution.py
@@ -20,6 +20,13 @@
 CHUNK = 16
 GROUP = 4
 DEPTH = 8
+PAIR_MAX = 2 * ROWB_MAX
+N_X = 4
+N_Z = 8
+N_CORE = 2
+PART = 80
+REST = TILE - PART
+MESH = pl.DeviceIdType.MESH
 
 VMEM = pltpu.MemorySpace.VMEM
 SMEM = pltpu.MemorySpace.SMEM
@@ -30,7 +37,7 @@
     return lax.shift_right_logical(value, jnp.full(value.shape, count, jnp.int32))
 
 
-def text_kernel(rows, cols, count, seed, tiles, out, acc, base):
+def text_kernel(rows, cols, count, seed, offsets, tiles, out, base):
     step = pl.program_id(0)
 
     @pl.when(step == 0)
@@ -39,15 +46,17 @@
         col_iota = lax.broadcasted_iota(jnp.int32, (TILE, SKETCH), 1)
         start = (row_iota * SKETCH + col_iota) ^ (seed[0] * 747796405)
         base[...] = start ^ shr(start, 16)
-        acc[...] = jnp.zeros_like(acc)
-
+        out[...] = jnp.zeros_like(out)
+
+    doc = lax.axis_index("doc")
+    first = offsets[doc] - offsets[doc - lax.rem(doc, 2)]
     slab = lax.axis_index("feat") * (TERMS // (TILE * N_FEAT))
     used = count[0]
 
-    def some(group, carry):
+    def some(width, first_at, group, carry):
         products = []
-        for lane in range(GROUP):
-            at = group * GROUP + lane
+        for lane in range(width):
+            at = first_at + group * width + lane
             block = (cols[step * CHUNK + at] + slab) * (TILE * SKETCH)
             block = block ^ lax.shift_right_logical(block, jnp.int32(16))
             mixing = base[...] ^ block
@@ -58,40 +67,37 @@
             levels = (shr(mixing, 8) & 65535).astype(jnp.float32)
             panel = ((levels - 32767.5) * (3.4641016 / 65536.0)).astype(jnp.bfloat16)
             products.append(jnp.dot(tiles[at], panel, preferred_element_type=jnp.float32))
-        for lane in range(GROUP):
-            at = step * CHUNK + group * GROUP + lane
-            place = jnp.where(at < used, rows[at], ROWB_MAX)
-            acc[place] += products[lane]
+        for lane in range(width):
+            at = step * CHUNK + first_at + group * width + lane
+            out[rows[at] + first] += products[lane]
         return carry
 
     left = jnp.clip(used - step * CHUNK, 0, CHUNK)
-    lax.fori_loop(0, (left + GROUP - 1) // GROUP, some, 0)
-
-    @pl.when(step == pl.num_programs(0) - 1)
-    def _():
-        out[...] = acc[0:ROWB_MAX]
-
-
-def text_stage(b_rows, b_cols, b_count, omega_seed, b_tiles):
+    whole = left // GROUP
+    lax.fori_loop(0, whole, functools.partial(some, GROUP, 0), 0)
+    lax.fori_loop(0, left - whole * GROUP, functools.partial(some, 1, whole * GROUP), 0)
+
+
+def text_stage(b_rows, b_cols, b_count, omega_seed, b_offsets, b_tiles):
     tiles_b = b_tiles.shape[0]
     return pl.pallas_call(
         text_kernel,
-        out_shape=jax.ShapeDtypeStruct((ROWB_MAX, TILE, SKETCH), jnp.float32),
+        out_shape=jax.ShapeDtypeStruct((PAIR_MAX, TILE, SKETCH), jnp.float32),
         grid=(tiles_b // CHUNK,),
         in_specs=[
             pl.BlockSpec(memory_space=SMEM),
             pl.BlockSpec(memory_space=SMEM),
             pl.BlockSpec(memory_space=SMEM),
             pl.BlockSpec(memory_space=SMEM),
+            pl.BlockSpec(memory_space=SMEM),
             pl.BlockSpec((CHUNK, TILE, TILE), lambda i: (i, 0, 0)),
         ],
-        out_specs=pl.BlockSpec((ROWB_MAX, TILE, SKETCH), lambda i: (0, 0, 0)),
+        out_specs=pl.BlockSpec((PAIR_MAX, TILE, SKETCH), lambda i: (0, 0, 0)),
         scratch_shapes=[
-            pltpu.VMEM((ROWB_MAX + 1, TILE, SKETCH), jnp.float32),
             pltpu.VMEM((TILE, SKETCH), jnp.int32),
         ],
         cost_estimate=pl.CostEstimate(flops=1700000000, bytes_accessed=8000000, transcendentals=0),
-    )(b_rows, b_cols, b_count, omega_seed, b_tiles)
+    )(b_rows, b_cols, b_count, omega_seed, b_offsets, b_tiles)
 
 
 def pack_kernel(tags, rows, count, tiles, outbox, meta, seen, notes, sems, meta_sem):
@@ -165,39 +171,403 @@
     )(a_tags, a_rows, a_count, a_tiles)
 
 
-def final_kernel(notes, b_offsets, a_offsets, inbox, gathered, out, lists, zbuf, sems):
+def exchange_kernel(
+    depth,
+    partial,
+    outbox,
+    main,
+    side,
+    inbox,
+    stage,
+    own,
+    core_in,
+    sums,
+    feat_in,
+    main_own,
+    side_own,
+    core_sem,
+    load_sem,
+    feat_sem,
+    place_sem,
+    z_sem,
+    second_sem,
+    third_sem,
+    pair_sem,
+    across_sem,
+    tiles_sem,
+    keep_sem,
+):
+    doc = lax.axis_index("doc")
+    feat = lax.axis_index("feat")
+    core = lax.rem(doc, N_CORE)
+    z = lax.rem(doc // N_CORE, N_Z)
+    x = doc // (N_CORE * N_Z)
+    lane = z * N_CORE + core
+
+    def device(x_to, z_to, core_to, feat_to):
+        return ((x_to * N_Z + z_to) * N_CORE + core_to, feat_to)
+
+    def turn(value, step, size):
+        return lax.rem(value + (step % size), size)
+
+    sibling = device(x, z, 1 - core, feat)
+
+    def remote(source, target, sems, to):
+        return pltpu.make_async_remote_copy(
+            src_ref=source,
+            dst_ref=target,
+            send_sem=sems[0],
+            recv_sem=sems[1],
+            device_id=to,
+            device_id_type=MESH,
+        )
+
+    barrier = pltpu.get_barrier_semaphore()
+
+    def greet(step, carry):
+        other = lax.rem(lane + step, N_Z * N_CORE)
+        pl.semaphore_signal(
+            barrier, inc=1, device_id=(x * (N_Z * N_CORE) + other, feat), device_id_type=MESH
+        )
+        return carry
+
+    lax.fori_loop(1, N_Z * N_CORE, greet, 0)
+    for step in range(1, N_X):
+        pl.semaphore_signal(
+            barrier, inc=1, device_id=device(turn(x, step, N_X), z, core, feat), device_id_type=MESH
+        )
+    for step in range(1, N_FEAT):
+        pl.semaphore_signal(
+            barrier, inc=1, device_id=device(x, z, core, turn(feat, step, N_FEAT)), device_id_type=MESH
+        )
+    pl.semaphore_wait(barrier, N_Z * N_CORE - 1 + N_X - 1 + N_FEAT - 1)
+
+    from_core = remote(
+        partial.at[pl.ds(0, depth), 1 - core], core_in, (core_sem.at[0], core_sem.at[1]), sibling
+    )
+    from_core.start()
+    load = pltpu.make_async_copy(partial.at[pl.ds(0, depth), core], own, load_sem)
+    load.start()
+
+    def across(step):
+        to = turn(x, step, N_X)
+        return remote(
+            outbox.at[to], stage.at[x], (across_sem.at[0, step], across_sem.at[1, step]),
+            device(to, z, core, feat),
+        )
+
+    for step in (1, 3, 2):
+        across(step).start()
+
+    load.wait()
+    from_core.wait()
+    for to in range(N_FEAT):
+        for k in range(depth):
+            sums[to, k] = own[k, to] + core_in[k, to]
+
+    def to_feat(step):
+        to = turn(feat, step, N_FEAT)
+        return remote(
+            sums.at[to], feat_in.at[step - 1], (feat_sem.at[0, step], feat_sem.at[1, step]),
+            device(x, z, core, to),
+        )
+
+    for step in (1, 3, 2):
+        to_feat(step).start()
+    for step in (1, 3, 2):
+        to_feat(step).wait_recv()
+    for k in range(depth):
+        row = ((sums[feat, k] + feat_in[0, k]) + (feat_in[1, k] + feat_in[2, k])).astype(jnp.bfloat16)
+        main_own[k] = row[:PART]
+        side_own[k] = row[PART:]
+
+    place_main = pltpu.make_async_copy(main_own, main.at[core, feat, x, z], place_sem.at[0])
+    place_side = pltpu.make_async_copy(side_own, side.at[core, x, feat, z], place_sem.at[1])
+    place_main.start()
+    place_side.start()
+
+    upper = depth // 2
+
+    def ring_z(way, which, step):
+        sign = 1 if way == 0 else -1
+        block = turn(z, -sign * (step - 1), N_Z)
+        held = main.at[core, feat, x, block] if which == 0 else side.at[core, x, feat, block]
+        source = held if step > 1 else (main_own if which == 0 else side_own)
+        if step == N_Z // 2:
+            part = pl.ds(0, upper) if way == 0 else pl.ds(upper, depth - upper)
+            held = held.at[part]
+            source = source.at[part]
+        return remote(
+            source, held, (z_sem.at[0, way, which, step], z_sem.at[1, way, which, step]),
+            device(x, turn(z, sign, N_Z), core, feat),
+        )
+
+    for step in range(1, N_Z // 2 + 1):
+        for way in range(2):
+            for which in range(2):
+                if step > 1:
+                    ring_z(way, which, step - 1).wait_recv()
+                ring_z(way, which, step).start()
+    for way in range(2):
+        for which in range(2):
+            ring_z(way, which, N_Z // 2).wait_recv()
+    place_main.wait()
+    place_side.wait()
+
+    half = N_Z // 2
+
+    def ring_four(sems, at, axis, block, kind):
+        way, part, hop = kind
+        sign = 1 if way == 0 else -1
+        if axis == 0:
+            place, to = x, device(turn(x, sign, N_X), z, core, feat)
+        else:
+            place, to = feat, device(x, z, core, turn(feat, sign, N_FEAT))
+        ref = block(turn(place, -sign * (hop - 1), 4)).at[pl.ds(part * half, half)]
+        number = way * 3 + (part ^ way if hop == 1 else 2)
+        return remote(ref, ref, (sems.at[0, at, number], sems.at[1, at, number]), to)
+
+    first_kinds = ((0, 0, 1), (1, 1, 1), (0, 1, 1), (1, 0, 1))
+    later_kinds = ((0, 0, 2), (1, 1, 2))
+
+    def main_block(feat_at, x_at):
+        return main.at[core, feat_at, x_at]
+
+    def side_block(x_at, feat_at):
+        return side.at[core, x_at, feat_at]
+
+    def second(which, kind):
+        if which == 0:
+            return ring_four(second_sem, 0, 0, lambda i: main_block(feat, i), kind)
+        return ring_four(second_sem, 1, 1, lambda i: side_block(x, i), kind)
+
+    def third(which, step, kind):
+        if which == 0:
+            chunk = turn(x, step, N_X)
+            return ring_four(third_sem, step, 1, lambda i: main_block(i, chunk), kind)
+        chunk = turn(feat, step, N_FEAT)
+        return ring_four(third_sem, 4 + step, 0, lambda i: side_block(i, chunk), kind)
+
+    def to_sibling(which, far, step):
+        if which == 0:
+            ref = main_block(turn(feat, far, N_FEAT), turn(x, step, N_X))
+        else:
+            ref = side_block(turn(x, far, N_X), turn(feat, step, N_FEAT))
+        at = which * 16 + far * 4 + step
+        return remote(ref, ref, (pair_sem.at[0, at], pair_sem.at[1, at]), sibling)
+
+    for kind in first_kinds:
+        second(1, kind).start()
+        second(0, kind).start()
+    for kind in first_kinds:
+        third(0, 0, kind).start()
+        third(1, 0, kind).start()
+    to_sibling(0, 0, 0).start()
+    to_sibling(1, 0, 0).start()
+
+    def tiles_to(step, source, from_x):
+        other = lax.rem(lane + step, N_Z * N_CORE)
+        return remote(
+            source.at[other], inbox.at[from_x, lane],
+            (tiles_sem.at[0, from_x, step], tiles_sem.at[1, from_x, step]),
+            (x * (N_Z * N_CORE) + other, feat),
+        )
+
+    def send_tiles(source, from_x, at):
+        def one(step, carry):
+            tiles_to(step, source, from_x).start()
+            return carry
+
+        lax.fori_loop(1, N_Z * N_CORE, one, 0)
+        pltpu.make_async_copy(source.at[lane], inbox.at[from_x, lane], keep_sem.at[at]).start()
+
+    send_tiles(outbox.at[x], x, 0)
+
+    def pass_on_second(which):
+        for kind in later_kinds:
+            way, part, _ = kind
+            second(which, (way, part, 1)).wait_recv()
+            second(which, kind).start()
+
+    def finish_second(which):
+        second(which, (0, 1, 1)).wait_recv()
+        for kind in first_kinds:
+            third(which, 3, kind).start()
+        to_sibling(which, 0, 3).start()
+        second(which, (1, 0, 1)).wait_recv()
+        for kind in first_kinds:
+            third(which, 1, kind).start()
+        to_sibling(which, 0, 1).start()
+
+    def finish_far(which):
+        for kind in later_kinds:
+            second(which, kind).wait_recv()
+        for kind in first_kinds:
+            third(which, 2, kind).start()
+        to_sibling(which, 0, 2).start()
+
+    def pass_on_third(which, step):
+        for kind in later_kinds:
+            way, part, _ = kind
+            third(which, step, (way, part, 1)).wait_recv()
+            third(which, step, kind).start()
+
+    def finish_third(which, step):
+        third(which, step, (0, 1, 1)).wait_recv()
+        to_sibling(which, 3, step).start()
+        third(which, step, (1, 0, 1)).wait_recv()
+        to_sibling(which, 1, step).start()
+        for kind in later_kinds:
+            third(which, step, kind).wait_recv()
+        to_sibling(which, 2, step).start()
+
+    pass_on_second(1)
+    pass_on_second(0)
+    finish_second(1)
+    pass_on_third(1, 0)
+    pass_on_third(0, 0)
+    finish_second(0)
+    finish_far(1)
+    finish_far(0)
+    for at, step in ((1, 1), (2, 3), (3, 2)):
+        across(step).wait_recv()
+        from_x = turn(x, -step, N_X)
+        send_tiles(stage.at[from_x], from_x, at)
+    finish_third(1, 0)
+    finish_third(0, 0)
+    for step in (3, 1, 2):
+        pass_on_third(1, step)
+        pass_on_third(0, step)
+        finish_third(1, step)
+        finish_third(0, step)
+
+    for which in range(2):
+        for far in range(4):
+            for step in range(4):
+                to_sibling(which, far, step).wait_recv()
+                to_sibling(which, far, step).wait_send()
+        for kind in first_kinds + later_kinds:
+            second(which, kind).wait_send()
+        for step in range(4):
+            for kind in first_kinds + later_kinds:
+                third(which, step, kind).wait_send()
+        for way in range(2):
+            for step in range(1, N_Z // 2 + 1):
+                ring_z(way, which, step).wait_send()
+    for step in (1, 2, 3):
+        to_feat(step).wait_send()
+        across(step).wait_send()
+
+    def settle(from_x, carry):
+        def one(step, inner):
+            copy = tiles_to(step, stage.at[0], from_x)
+            copy.wait_recv()
+            copy.wait_send()
+            return inner
+
+        lax.fori_loop(1, N_Z * N_CORE, one, 0)
+        pltpu.make_async_copy(stage.at[0, 0], inbox.at[0, 0], keep_sem.at[from_x]).wait()
+        return carry
+
+    lax.fori_loop(0, N_X, settle, 0)
+
+
+def exchange_stage(depth, partial, outbox):
+    bf16 = jnp.bfloat16
+    dma = pltpu.SemaphoreType.DMA
+    wide = N_Z * N_CORE
+    block = (TILE, SKETCH)
+    main, side, inbox, _ = pl.pallas_call(
+        functools.partial(exchange_kernel, depth),
+        out_shape=(
+            jax.ShapeDtypeStruct((N_CORE, N_FEAT, N_X, N_Z, depth, PART, SKETCH), bf16),
+            jax.ShapeDtypeStruct((N_CORE, N_X, N_FEAT, N_Z, depth, REST, SKETCH), bf16),
+            jax.ShapeDtypeStruct((N_X, wide, PAGE, TILE), bf16),
+            jax.ShapeDtypeStruct((N_X, wide, PAGE, TILE), bf16),
+        ),
+        in_specs=[pl.BlockSpec(memory_space=ANY)] * 2,
+        out_specs=(pl.BlockSpec(memory_space=ANY),) * 4,
+        scratch_shapes=[
+            pltpu.VMEM((depth, N_FEAT) + block, jnp.float32),
+            pltpu.VMEM((depth, N_FEAT) + block, jnp.float32),
+            pltpu.VMEM((N_FEAT, depth) + block, jnp.float32),
+            pltpu.VMEM((N_FEAT - 1, depth) + block, jnp.float32),
+            pltpu.VMEM((depth, PART, SKETCH), bf16),
+            pltpu.VMEM((depth, REST, SKETCH), bf16),
+            dma((2,)),
+            dma,
+            dma((2, 4)),
+            dma((2,)),
+            dma((2, 2, 2, N_Z // 2 + 1)),
+            dma((2, 2, 6)),
+            dma((2, 8, 6)),
+            dma((2, 32)),
+            dma((2, 4)),
+            dma((2, N_X, wide)),
+            dma((4,)),
+        ],
+        compiler_params=pltpu.CompilerParams(collective_id=depth, has_side_effects=True),
+        name="exchange_%d" % depth,
+    )(
+        partial.reshape(PAIR_MAX // 8, N_CORE, N_FEAT, TILE, SKETCH),
+        outbox.reshape(N_X, wide, PAGE, TILE),
+    )
+    count = N_CORE * N_FEAT * N_X * N_Z * depth
+    return (
+        main.reshape(count, PART, SKETCH),
+        side.reshape(count, REST, SKETCH),
+        inbox.reshape(N_DOC, PAGE, TILE),
+    )
+
+
+def final_kernel(
+    depth, notes, b_offsets, a_offsets, inbox, main, side, out, lists, zbuf, main_sems, side_sems
+):
     def listed(doc, found):
-        shift = a_offsets[doc] - b_offsets[doc]
-        before = b_offsets[doc] - b_offsets[jnp.maximum(doc - 1, 0)]
         for rank in range(2):
             tag = notes[doc * 4 + rank * 2] - 1
-            row = notes[doc * 4 + rank * 2 + 1] + shift
-            index = jnp.where(
-                row < 0, (doc - 1) * ROWB_MAX + row + before, doc * ROWB_MAX + row
-            )
+            row = notes[doc * 4 + rank * 2 + 1] + a_offsets[doc]
+            owner = jnp.maximum(doc - (row < b_offsets[doc]).astype(jnp.int32), 0)
+            chip = lax.shift_right_logical(owner, jnp.int32(1))
+            inner = jnp.clip(row - b_offsets[chip * 2], 0, depth * 8 - 1)
+            k = lax.shift_right_logical(inner, jnp.int32(3))
+            core = lax.shift_right_logical(inner, jnp.int32(2)) & 1
+            feat = inner & 3
+            x = lax.shift_right_logical(chip, jnp.int32(3))
+            z = chip & 7
             lists[0, found] = tag
-            lists[1, found] = jnp.maximum(index, 0)
-            lists[2, found] = doc * 2 + rank
+            lists[1, found] = (((core * N_FEAT + feat) * N_X + x) * N_Z + z) * depth + k
+            lists[2, found] = (((core * N_X + x) * N_FEAT + feat) * N_Z + z) * depth + k
+            lists[3, found] = doc * 2 + rank
             found = found + (tag >= 0).astype(jnp.int32)
         return found
 
     total = lax.fori_loop(0, N_DOC, listed, 0)
 
     def fetch(at, slot):
-        return pltpu.make_async_copy(gathered.at[lists[1, at]], zbuf.at[slot], sems.at[slot])
+        return (
+            pltpu.make_async_copy(
+                main.at[lists[1, at]], zbuf.at[slot, pl.ds(0, PART)], main_sems.at[slot]
+            ),
+            pltpu.make_async_copy(
+                side.at[lists[2, at]], zbuf.at[slot, pl.ds(PART, REST)], side_sems.at[slot]
+            ),
+        )
 
     for first in range(DEPTH):
 
         @pl.when(first < total)
         def _():
-            fetch(first, first).start()
+            for copy in fetch(first, first):
+                copy.start()
 
     out[...] = jnp.zeros_like(out)
 
     def add(at, carry):
         slot = lax.rem(at, DEPTH)
-        fetch(at, slot).wait()
-        source = lists[2, at]
+        for copy in fetch(at, slot):
+            copy.wait()
+        source = lists[3, at]
         start = pl.multiple_of((source & 1) * TILE, TILE)
         tile = inbox[lax.shift_right_logical(source, jnp.int32(1)), pl.ds(start, TILE), :]
         product = lax.dot_general(
@@ -208,31 +578,34 @@
 
         @pl.when(at + DEPTH < total)
         def _():
-            fetch(at + DEPTH, slot).start()
+            for copy in fetch(at + DEPTH, slot):
+                copy.start()
 
         return carry
 
     lax.fori_loop(0, total, add, 0)
 
 
-def final_stage(notes, b_offsets, a_offsets, inbox, gathered):
+def final_stage(depth, notes, b_offsets, a_offsets, inbox, main, side):
     return pl.pallas_call(
-        final_kernel,
+        functools.partial(final_kernel, depth),
         out_shape=jax.ShapeDtypeStruct((TAG_DEV, SKETCH), jnp.float32),
         in_specs=[
             pl.BlockSpec(memory_space=SMEM),
             pl.BlockSpec(memory_space=SMEM),
             pl.BlockSpec(memory_space=SMEM),
             pl.BlockSpec(memory_space=VMEM),
+            pl.BlockSpec(memory_space=ANY),
             pl.BlockSpec(memory_space=ANY),
         ],
         out_specs=pl.BlockSpec(memory_space=VMEM),
         scratch_shapes=[
-            pltpu.SMEM((3, 2 * N_DOC + 1), jnp.int32),
+            pltpu.SMEM((4, 2 * N_DOC + 1), jnp.int32),
             pltpu.VMEM((DEPTH, TILE, SKETCH), jnp.bfloat16),
             pltpu.SemaphoreType.DMA((DEPTH,)),
+            pltpu.SemaphoreType.DMA((DEPTH,)),
         ],
-    )(notes, b_offsets, a_offsets, inbox, gathered)
+    )(notes, b_offsets, a_offsets, inbox, main, side)
 
 
 def local(
@@ -249,17 +622,16 @@
     omega_seed,
 ):
     outbox = pack_stage(a_tags[:, 0], a_rows[:, 0], a_count[:, 0], a_tiles)
-    inbox = lax.all_to_all(outbox, "doc", split_axis=0, concat_axis=0, tiled=True)
-    partial = text_stage(b_rows[:, 0], b_cols[:, 0], b_count[:, 0], omega_seed, b_tiles)
-    mine = lax.psum_scatter(partial, "feat", scatter_dimension=0, tiled=True)
-    gathered = lax.all_gather(mine.astype(jnp.bfloat16), ("doc", "feat"))
-    notes = inbox[:, 2 * TILE, 0:4].astype(jnp.int32).reshape(-1)
-    return final_stage(
-        notes,
-        b_offsets,
-        a_offsets,
-        inbox,
-        gathered.reshape(N_DOC * ROWB_MAX, TILE, SKETCH),
+    partial = text_stage(b_rows[:, 0], b_cols[:, 0], b_count[:, 0], omega_seed, b_offsets, b_tiles)
+
+    def rest(depth, partial, outbox):
+        main, side, inbox = exchange_stage(depth, partial, outbox)
+        notes = inbox[:, 2 * TILE, 0:4].astype(jnp.int32).reshape(-1)
+        return final_stage(depth, notes, b_offsets, a_offsets, inbox, main, side)
+
+    most = jnp.max(b_offsets[2::2] - b_offsets[:-1:2])
+    return lax.cond(
+        most <= 16, functools.partial(rest, 2), functools.partial(rest, 3), partial, outbox
     )
 
 

time: 333 us -> 228 us (0.68)
  Pallas kernels: 49.4 us -> 218 us
  blocking collectives: 137 us -> 0 us
  waiting for transfers between devices: 122 us -> 0 us
  between operations: 15.4 us -> 2.65 us
    pallas_call x2 -> x3, Pallas kernels: 44.5 us -> 213 us  [the longest x1 167 us: exchange_stage(): pl.pallas_call(functools.partial(exchange_kernel, depth), out_shape=(jax....]
    all_to_all x1 -> x0, blocking collectives: 137 us -> none  [local(): lax.all_to_all(outbox, 'doc', split_axis=0, concat_axis=0, tiled=True)]
    all_gather x1 -> x0, waiting for transfers between devices: 90.9 us -> none  [local(): gathered = lax.all_gather(mine.astype(jnp.bfloat16), ('doc', 'feat'))]
    reduce_scatter x1 -> x0, waiting for transfers between devices: 31.3 us -> none  [local(): mine = lax.psum_scatter(partial, 'feat', scatter_dimension=0, tiled=True)]
  transfers between devices with their start and end apart: 2 -> 0, of which waited for: 2 -> 0; matrix products, arithmetic and copies ran while one was open for 0% -> 0% of each run, Pallas kernels for 1% -> 0%
where the time goes in v2:
time: 228 us; the launch traced here: 225 us
  Pallas kernels  218 us (96%)
  between operations  2.65 us (1%)
    pallas_call x1, Pallas kernels, exchange_stage(): pl.pallas_call(functools.partial(exchange_kernel, depth), out_shape=(jax....  167 us
    pallas_call x1, Pallas kernels, final_stage(): pl.pallas_call(functools.partial(final_kernel, depth), out_shape=jax.Shap...  27.4 us
    pallas_call x1, Pallas kernels, text_stage(): pl.pallas_call(text_kernel, out_shape=jax.ShapeDtypeStruct((PAIR_MAX, TIL...  19.2 us
    pallas_call x1, Pallas kernels, pack_stage(): pl.pallas_call(pack_kernel, out_shape=jax.ShapeDtypeStruct((N_DOC, PAGE,...  4.91 us

profile of v2, /device:TPU:24, one launch (start us, length us, event | category | flops | bytes accessed | tf_op | source)
XLA Modules:
  0.0 224.7 jit_solution(860203373319530981)
XLA Ops:
  1.9 0.8 slice.13
  2.7 0.8 slice.12
  3.5 0.6 subtract_reduce_fusion
  4.8 19.2 %shard_map.113 = f32[24,128,256]{2,1,0:T(8,128)S(1)} custom-call(s32[192]{0:T(256)} %bitcast.30, s32[192]{0:T(256)} %bitcast.31, s32[1]{0:T(128)} %bitcast.16.count, s32[1]{0:T(128)S(6)} %copy.20.seed, s32[65]{0:T(128)} %offsets.1, bf16[192,128,128]{2,1,0:T(8,128)(2,1)} %tiles.2), custom_call_target="tpu_custom_call" | custom-call | flops 1700000000 | bytes 8000000 | tf_op jit(solution)/shard_map/pallas_call | solution.py:83
  24.0 0.0 copy-start
  24.0 0.0 copy-start.1
  24.0 4.9 %shard_map.114 = bf16[64,272,128]{2,1,0:T(8,128)(2,1)} custom-call(s32[64]{0:T(128)} %bitcast.32, s32[64]{0:T(128)} %bitcast.33, s32[1]{0:T(128)} %bitcast.17.count, bf16[64,128,128]{2,1,0:T(8,128)(2,1)} %tiles.3), custom_call_target="tpu_custom_call" | custom-call | tf_op jit(solution)/shard_map/pallas_call | solution.py:154
  28.9 0.0 copy-done
  28.9 0.0 copy-done.1
  29.0 195.7 %conditional.1 = (f32[4096,256]{1,0:T(8,128)}) conditional(s32[]{:T(128)} %convert_element_type.17, (f32[24,128,256]{2,1,0:T(8,128)S(1)}, bf16[64,272,128]{2,1,0:T(8,128)(2,1)}, s32[65]{0:T(128)S(1)}, s32[65]{0:T(128)S(1)}) %tuple.18, (f32[24,128,256]{2,1,0:T(8,128)S(1)}, bf16[64,272,128]{2,1,0:T(8,128)(2,1)}, s32[65]{0:T(128)S(1)}, ...), branch_computations={%region_1.0_spmd, %region_2.0_spmd} | conditional | flops 256 | bytes 3592 | solution.py:633
  29.0 166.6 %exchange_2.1 = (bf16[2,4,4,8,2,80,256]{6,5,4,3,2,1,0:T(8,128)(2,1)}, bf16[2,4,4,8,2,48,256]{6,5,4,3,2,1,0:T(8,128)(2,1)}, bf16[4,16,272,128]{3,2,1,0:T(8,128)(2,1)}, bf16[4,16,272,128]{3,2,1,0:T(8,128)(2,1)}) custom-call(f32[3,2,4,128,256]{4,3,2,1,0:T(8,128)S(1)} %bitcast.22, bf16[4,16,272,128]{3,2,1,0:T(8,128)(2,1)} %bitcast.19), custom_call_target="tpu_custom_call" | custom-call | tf_op jit(solution)/shard_map/cond/branch_1_fun/exchange_2/pallas_call | solution.py:480
  195.6 1.0 fusion.1
  196.6 0.7 reshape.39.notes
  197.3 27.4 %branch_1_fun.1 = f32[4096,256]{1,0:T(8,128)} custom-call(s32[256]{0:T(256)} %reshape.39.notes, s32[65]{0:T(128)S(1)} %get-tuple-element.34.b_offsets, s32[65]{0:T(128)S(1)} %get-tuple-element.42.a_offsets, bf16[64,272,128]{2,1,0:T(8,128)(2,1)} %bitcast.29, bf16[512,80,256]{2,1,0:T(8,128)(2,1)} %bitcast.23, bf16[512,48,256]{2,1,0:T(8,128)(2,1)} %bitcast.25), custom_call_target="tpu_custom_call" | custom-call | tf_op jit(solution)/shard_map/cond/branch_1_fun/pallas_call | solution.py:590
Async XLA Ops:
  24.0 4.9 %copy-start = (s32[65]{0:T(128)S(1)}, s32[65]{0:T(128)}, u32[]{:S(2)}) copy-start(s32[65]{0:T(128)} %offsets.1) | copy-start | bytes 784
  24.0 4.9 %copy-start.1 = (s32[65]{0:T(128)S(1)}, s32[65]{0:T(128)}, u32[]{:S(2)}) copy-start(s32[65]{0:T(128)} %param.22) | copy-start | bytes 784

commit v3 on v2

--- a/solution.py
+++ b/solution.py
@@ -19,13 +19,12 @@
 PAGE = 2 * TILE + META
 CHUNK = 16
 GROUP = 4
-DEPTH = 8
+TOGETHER = 4
+DEPTH = 2 * N_DOC
 PAIR_MAX = 2 * ROWB_MAX
 N_X = 4
 N_Z = 8
 N_CORE = 2
-PART = 80
-REST = TILE - PART
 MESH = pl.DeviceIdType.MESH
 
 VMEM = pltpu.MemorySpace.VMEM
@@ -37,16 +36,76 @@
     return lax.shift_right_logical(value, jnp.full(value.shape, count, jnp.int32))
 
 
-def text_kernel(rows, cols, count, seed, offsets, tiles, out, base):
+def text_kernel(
+    rows, cols, count, seed, offsets, tags, tag_rows, tag_count, tiles, tag_tiles,
+    out, outbox,
+    acc, base, held, meta, seen, notes, slots, load_sem, sems, meta_sem,
+):
     step = pl.program_id(0)
+    used_tags = tag_count[0]
+
+    def load():
+        return pltpu.make_async_copy(tag_tiles, held, load_sem)
+
+    def put(at, owner, rank):
+        start = pl.multiple_of(rank * TILE, TILE)
+        return pltpu.make_async_copy(
+            held.at[at], outbox.at[owner, pl.ds(start, TILE), :], sems.at[at]
+        )
+
+    def put_meta():
+        return pltpu.make_async_copy(meta, outbox.at[:, pl.ds(2 * TILE, META), :], meta_sem)
 
     @pl.when(step == 0)
     def _():
+        load().start()
         row_iota = lax.broadcasted_iota(jnp.int32, (TILE, SKETCH), 0)
         col_iota = lax.broadcasted_iota(jnp.int32, (TILE, SKETCH), 1)
         start = (row_iota * SKETCH + col_iota) ^ (seed[0] * 747796405)
         base[...] = start ^ shr(start, 16)
-        out[...] = jnp.zeros_like(out)
+        acc[...] = jnp.zeros_like(acc)
+
+        def clear(owner, carry):
+            seen[owner] = 0
+            for lane in range(4):
+                notes[owner * 4 + lane] = 0
+            return carry
+
+        lax.fori_loop(0, N_DOC, clear, 0)
+
+        def sort(at, carry):
+            tag = tags[at]
+            owner = lax.shift_right_logical(tag, jnp.int32(7))
+            rank = jnp.minimum(seen[owner], 1)
+            seen[owner] = rank + 1
+            notes[owner * 4 + rank * 2] = (tag & (OWNED - 1)) + 1
+            notes[owner * 4 + rank * 2 + 1] = tag_rows[at]
+            slots[at] = owner * 2 + rank
+            return carry
+
+        lax.fori_loop(0, used_tags, sort, 0)
+
+    @pl.when(step == 1)
+    def _():
+        load().wait()
+
+        def send(at, carry):
+            slot = slots[at]
+            put(at, lax.shift_right_logical(slot, jnp.int32(1)), slot & 1).start()
+            return carry
+
+        lax.fori_loop(0, used_tags, send, 0)
+        lane_iota = lax.broadcasted_iota(jnp.int32, (META, TILE), 1)
+
+        def note(owner, carry):
+            value = jnp.zeros((META, TILE), jnp.int32)
+            for lane in range(4):
+                value = jnp.where(lane_iota == lane, notes[owner * 4 + lane], value)
+            meta[owner] = value.astype(jnp.float32).astype(jnp.bfloat16)
+            return carry
+
+        lax.fori_loop(0, N_DOC, note, 0)
+        put_meta().start()
 
     doc = lax.axis_index("doc")
     first = offsets[doc] - offsets[doc - lax.rem(doc, 2)]
@@ -69,7 +128,7 @@
             products.append(jnp.dot(tiles[at], panel, preferred_element_type=jnp.float32))
         for lane in range(width):
             at = step * CHUNK + first_at + group * width + lane
-            out[rows[at] + first] += products[lane]
+            acc[rows[at] + first] += products[lane]
         return carry
 
     left = jnp.clip(used - step * CHUNK, 0, CHUNK)
@@ -77,98 +136,52 @@
     lax.fori_loop(0, whole, functools.partial(some, GROUP, 0), 0)
     lax.fori_loop(0, left - whole * GROUP, functools.partial(some, 1, whole * GROUP), 0)
 
-
-def text_stage(b_rows, b_cols, b_count, omega_seed, b_offsets, b_tiles):
-    tiles_b = b_tiles.shape[0]
+    @pl.when(step == pl.num_programs(0) - 1)
+    def _():
+        out[...] = acc[...].astype(jnp.bfloat16)
+
+        def drain(at, carry):
+            put(at, 0, 0).wait()
+            return carry
+
+        lax.fori_loop(0, used_tags, drain, 0)
+        put_meta().wait()
+
+
+def text_stage(b_rows, b_cols, b_count, omega_seed, b_offsets, a_tags, a_rows, a_count, b_tiles, a_tiles):
+    tiles_b, tiles_a = b_tiles.shape[0], a_tiles.shape[0]
+    rows_shape = (PAIR_MAX, TILE, SKETCH)
     return pl.pallas_call(
         text_kernel,
-        out_shape=jax.ShapeDtypeStruct((PAIR_MAX, TILE, SKETCH), jnp.float32),
+        out_shape=(
+            jax.ShapeDtypeStruct(rows_shape, jnp.bfloat16),
+            jax.ShapeDtypeStruct((N_DOC, PAGE, TILE), jnp.bfloat16),
+        ),
         grid=(tiles_b // CHUNK,),
-        in_specs=[
-            pl.BlockSpec(memory_space=SMEM),
-            pl.BlockSpec(memory_space=SMEM),
-            pl.BlockSpec(memory_space=SMEM),
-            pl.BlockSpec(memory_space=SMEM),
-            pl.BlockSpec(memory_space=SMEM),
+        in_specs=[pl.BlockSpec(memory_space=SMEM)] * 8
+        + [
             pl.BlockSpec((CHUNK, TILE, TILE), lambda i: (i, 0, 0)),
+            pl.BlockSpec(memory_space=ANY),
         ],
-        out_specs=pl.BlockSpec((PAIR_MAX, TILE, SKETCH), lambda i: (0, 0, 0)),
+        out_specs=(
+            pl.BlockSpec(rows_shape, lambda i: (0, 0, 0)),
+            pl.BlockSpec(memory_space=ANY),
+        ),
         scratch_shapes=[
+            pltpu.VMEM(rows_shape, jnp.float32),
             pltpu.VMEM((TILE, SKETCH), jnp.int32),
-        ],
-        cost_estimate=pl.CostEstimate(flops=1700000000, bytes_accessed=8000000, transcendentals=0),
-    )(b_rows, b_cols, b_count, omega_seed, b_offsets, b_tiles)
-
-
-def pack_kernel(tags, rows, count, tiles, outbox, meta, seen, notes, sems, meta_sem):
-    used = count[0]
-
-    def clear(owner, carry):
-        seen[owner] = 0
-        for lane in range(4):
-            notes[owner * 4 + lane] = 0
-        return carry
-
-    lax.fori_loop(0, N_DOC, clear, 0)
-
-    def copy(at, owner, rank):
-        start = pl.multiple_of(rank * TILE, TILE)
-        return pltpu.make_async_copy(
-            tiles.at[at], outbox.at[owner, pl.ds(start, TILE), :], sems.at[at]
-        )
-
-    def send(at, carry):
-        tag = tags[at]
-        owner = lax.shift_right_logical(tag, jnp.int32(7))
-        rank = jnp.minimum(seen[owner], 1)
-        seen[owner] = rank + 1
-        notes[owner * 4 + rank * 2] = (tag & (OWNED - 1)) + 1
-        notes[owner * 4 + rank * 2 + 1] = rows[at]
-        copy(at, owner, rank).start()
-        return carry
-
-    lax.fori_loop(0, used, send, 0)
-    lane_iota = lax.broadcasted_iota(jnp.int32, (META, TILE), 1)
-
-    def note(owner, carry):
-        value = jnp.zeros((META, TILE), jnp.int32)
-        for lane in range(4):
-            value = jnp.where(lane_iota == lane, notes[owner * 4 + lane], value)
-        meta[owner] = value.astype(jnp.float32).astype(jnp.bfloat16)
-        return carry
-
-    lax.fori_loop(0, N_DOC, note, 0)
-    last = pltpu.make_async_copy(meta, outbox.at[:, pl.ds(2 * TILE, META), :], meta_sem)
-    last.start()
-
-    def drain(at, carry):
-        copy(at, 0, 0).wait()
-        return carry
-
-    lax.fori_loop(0, used, drain, 0)
-    last.wait()
-
-
-def pack_stage(a_tags, a_rows, a_count, a_tiles):
-    tiles_a = a_tiles.shape[0]
-    return pl.pallas_call(
-        pack_kernel,
-        out_shape=jax.ShapeDtypeStruct((N_DOC, PAGE, TILE), jnp.bfloat16),
-        in_specs=[
-            pl.BlockSpec(memory_space=SMEM),
-            pl.BlockSpec(memory_space=SMEM),
-            pl.BlockSpec(memory_space=SMEM),
-            pl.BlockSpec(memory_space=VMEM),
-        ],
-        out_specs=pl.BlockSpec(memory_space=ANY),
-        scratch_shapes=[
+            pltpu.VMEM((tiles_a, TILE, TILE), jnp.bfloat16),
             pltpu.VMEM((N_DOC, META, TILE), jnp.bfloat16),
             pltpu.SMEM((N_DOC,), jnp.int32),
             pltpu.SMEM((N_DOC * 4,), jnp.int32),
+            pltpu.SMEM((tiles_a,), jnp.int32),
+            pltpu.SemaphoreType.DMA,
             pltpu.SemaphoreType.DMA((tiles_a,)),
             pltpu.SemaphoreType.DMA,
         ],
-    )(a_tags, a_rows, a_count, a_tiles)
+        cost_estimate=pl.CostEstimate(flops=1700000000, bytes_accessed=8000000, transcendentals=0),
+        name="text",
+    )(b_rows, b_cols, b_count, omega_seed, b_offsets, a_tags, a_rows, a_count, b_tiles, a_tiles)
 
 
 def exchange_kernel(
@@ -197,6 +210,7 @@
     tiles_sem,
     keep_sem,
 ):
+    count = main.shape[4]
     doc = lax.axis_index("doc")
     feat = lax.axis_index("feat")
     core = lax.rem(doc, N_CORE)
@@ -259,6 +273,24 @@
     for step in (1, 3, 2):
         across(step).start()
 
+    def tiles_to(step, source, from_x):
+        other = lax.rem(lane + step, N_Z * N_CORE)
+        return remote(
+            source.at[other], inbox.at[from_x, lane],
+            (tiles_sem.at[0, from_x, step], tiles_sem.at[1, from_x, step]),
+            (x * (N_Z * N_CORE) + other, feat),
+        )
+
+    def send_tiles(source, from_x, at):
+        def one(step, carry):
+            tiles_to(step, source, from_x).start()
+            return carry
+
+        lax.fori_loop(1, N_Z * N_CORE, one, 0)
+        pltpu.make_async_copy(source.at[lane], inbox.at[from_x, lane], keep_sem.at[at]).start()
+
+    send_tiles(outbox.at[x], x, 0)
+
     load.wait()
     from_core.wait()
     for to in range(N_FEAT):
@@ -277,16 +309,19 @@
     for step in (1, 3, 2):
         to_feat(step).wait_recv()
     for k in range(depth):
-        row = ((sums[feat, k] + feat_in[0, k]) + (feat_in[1, k] + feat_in[2, k])).astype(jnp.bfloat16)
-        main_own[k] = row[:PART]
-        side_own[k] = row[PART:]
+        terms = [block[k].astype(jnp.float32) for block in (sums.at[feat], feat_in.at[0], feat_in.at[1], feat_in.at[2])]
+        row = ((terms[0] + terms[1]) + (terms[2] + terms[3])).astype(jnp.bfloat16)
+        if k < count:
+            main_own[k] = row
+        else:
+            side_own[k - count] = row
 
     place_main = pltpu.make_async_copy(main_own, main.at[core, feat, x, z], place_sem.at[0])
     place_side = pltpu.make_async_copy(side_own, side.at[core, x, feat, z], place_sem.at[1])
     place_main.start()
     place_side.start()
 
-    upper = depth // 2
+    upper = TILE // 2
 
     def ring_z(way, which, step):
         sign = 1 if way == 0 else -1
@@ -294,9 +329,9 @@
         held = main.at[core, feat, x, block] if which == 0 else side.at[core, x, feat, block]
         source = held if step > 1 else (main_own if which == 0 else side_own)
         if step == N_Z // 2:
-            part = pl.ds(0, upper) if way == 0 else pl.ds(upper, depth - upper)
-            held = held.at[part]
-            source = source.at[part]
+            part = pl.ds(way * upper, upper)
+            held = held.at[:, part]
+            source = source.at[:, part]
         return remote(
             source, held, (z_sem.at[0, way, which, step], z_sem.at[1, way, which, step]),
             device(x, turn(z, sign, N_Z), core, feat),
@@ -365,24 +400,6 @@
     to_sibling(0, 0, 0).start()
     to_sibling(1, 0, 0).start()
 
-    def tiles_to(step, source, from_x):
-        other = lax.rem(lane + step, N_Z * N_CORE)
-        return remote(
-            source.at[other], inbox.at[from_x, lane],
-            (tiles_sem.at[0, from_x, step], tiles_sem.at[1, from_x, step]),
-            (x * (N_Z * N_CORE) + other, feat),
-        )
-
-    def send_tiles(source, from_x, at):
-        def one(step, carry):
-            tiles_to(step, source, from_x).start()
-            return carry
-
-        lax.fori_loop(1, N_Z * N_CORE, one, 0)
-        pltpu.make_async_copy(source.at[lane], inbox.at[from_x, lane], keep_sem.at[at]).start()
-
-    send_tiles(outbox.at[x], x, 0)
-
     def pass_on_second(which):
         for kind in later_kinds:
             way, part, _ = kind
@@ -421,18 +438,22 @@
             third(which, step, kind).wait_recv()
         to_sibling(which, 2, step).start()
 
-    pass_on_second(1)
-    pass_on_second(0)
-    finish_second(1)
-    pass_on_third(1, 0)
-    pass_on_third(0, 0)
-    finish_second(0)
-    finish_far(1)
-    finish_far(0)
-    for at, step in ((1, 1), (2, 3), (3, 2)):
+    def send_across(at, step):
         across(step).wait_recv()
         from_x = turn(x, -step, N_X)
         send_tiles(stage.at[from_x], from_x, at)
+
+    pass_on_second(1)
+    pass_on_second(0)
+    send_across(1, 1)
+    send_across(2, 3)
+    finish_second(1)
+    finish_second(0)
+    pass_on_third(1, 0)
+    pass_on_third(0, 0)
+    send_across(3, 2)
+    finish_far(1)
+    finish_far(0)
     finish_third(1, 0)
     finish_third(0, 0)
     for step in (3, 1, 2):
@@ -477,23 +498,24 @@
     dma = pltpu.SemaphoreType.DMA
     wide = N_Z * N_CORE
     block = (TILE, SKETCH)
+    first = (depth + 1) // 2
     main, side, inbox, _ = pl.pallas_call(
         functools.partial(exchange_kernel, depth),
         out_shape=(
-            jax.ShapeDtypeStruct((N_CORE, N_FEAT, N_X, N_Z, depth, PART, SKETCH), bf16),
-            jax.ShapeDtypeStruct((N_CORE, N_X, N_FEAT, N_Z, depth, REST, SKETCH), bf16),
+            jax.ShapeDtypeStruct((N_CORE, N_FEAT, N_X, N_Z, first) + block, bf16),
+            jax.ShapeDtypeStruct((N_CORE, N_X, N_FEAT, N_Z, depth - first) + block, bf16),
             jax.ShapeDtypeStruct((N_X, wide, PAGE, TILE), bf16),
             jax.ShapeDtypeStruct((N_X, wide, PAGE, TILE), bf16),
         ),
         in_specs=[pl.BlockSpec(memory_space=ANY)] * 2,
         out_specs=(pl.BlockSpec(memory_space=ANY),) * 4,
         scratch_shapes=[
-            pltpu.VMEM((depth, N_FEAT) + block, jnp.float32),
-            pltpu.VMEM((depth, N_FEAT) + block, jnp.float32),
-            pltpu.VMEM((N_FEAT, depth) + block, jnp.float32),
-            pltpu.VMEM((N_FEAT - 1, depth) + block, jnp.float32),
-            pltpu.VMEM((depth, PART, SKETCH), bf16),
-            pltpu.VMEM((depth, REST, SKETCH), bf16),
+            pltpu.VMEM((depth, N_FEAT) + block, bf16),
+            pltpu.VMEM((depth, N_FEAT) + block, bf16),
+            pltpu.VMEM((N_FEAT, depth) + block, bf16),
+            pltpu.VMEM((N_FEAT - 1, depth) + block, bf16),
+            pltpu.VMEM((first,) + block, bf16),
+            pltpu.VMEM((depth - first,) + block, bf16),
             dma((2,)),
             dma,
             dma((2, 4)),
@@ -512,78 +534,93 @@
         partial.reshape(PAIR_MAX // 8, N_CORE, N_FEAT, TILE, SKETCH),
         outbox.reshape(N_X, wide, PAGE, TILE),
     )
-    count = N_CORE * N_FEAT * N_X * N_Z * depth
     return (
-        main.reshape(count, PART, SKETCH),
-        side.reshape(count, REST, SKETCH),
+        main.reshape((-1,) + block),
+        side.reshape((-1,) + block),
         inbox.reshape(N_DOC, PAGE, TILE),
     )
 
 
 def final_kernel(
-    depth, notes, b_offsets, a_offsets, inbox, main, side, out, lists, zbuf, main_sems, side_sems
+    depth, notes, b_offsets, a_offsets, inbox, main, side, out, lists, zbuf, sems
 ):
+    first_count = (depth + 1) // 2
+
+    def fetch(ref, at, slot):
+        group = lax.shift_right_logical(slot, jnp.int32(2))
+        return pltpu.make_async_copy(ref.at[at], zbuf.at[slot], sems.at[group])
+
     def listed(doc, found):
+        shift = a_offsets[doc]
+        split = b_offsets[doc]
+        before = jnp.maximum(doc - 1, 0)
+        chips = [lax.shift_right_logical(at, jnp.int32(1)) for at in (before, doc)]
+        bases = [shift - b_offsets[chip * 2] for chip in chips]
         for rank in range(2):
             tag = notes[doc * 4 + rank * 2] - 1
-            row = notes[doc * 4 + rank * 2 + 1] + a_offsets[doc]
-            owner = jnp.maximum(doc - (row < b_offsets[doc]).astype(jnp.int32), 0)
-            chip = lax.shift_right_logical(owner, jnp.int32(1))
-            inner = jnp.clip(row - b_offsets[chip * 2], 0, depth * 8 - 1)
-            k = lax.shift_right_logical(inner, jnp.int32(3))
-            core = lax.shift_right_logical(inner, jnp.int32(2)) & 1
-            feat = inner & 3
-            x = lax.shift_right_logical(chip, jnp.int32(3))
-            z = chip & 7
-            lists[0, found] = tag
-            lists[1, found] = (((core * N_FEAT + feat) * N_X + x) * N_Z + z) * depth + k
-            lists[2, found] = (((core * N_X + x) * N_FEAT + feat) * N_Z + z) * depth + k
-            lists[3, found] = doc * 2 + rank
+
+            @pl.when(tag >= 0)
+            def _():
+                row = notes[doc * 4 + rank * 2 + 1]
+                early = row + shift < split
+                chip = jnp.where(early, chips[0], chips[1])
+                inner = jnp.clip(row + jnp.where(early, bases[0], bases[1]), 0, depth * 8 - 1)
+                k = lax.shift_right_logical(inner, jnp.int32(3))
+                core = lax.shift_right_logical(inner, jnp.int32(2)) & 1
+                feat = inner & 3
+                x = lax.shift_right_logical(chip, jnp.int32(3))
+                z = chip & 7
+                lists[0, found] = tag
+                lists[1, found] = doc * 2 + rank
+
+                @pl.when(k < first_count)
+                def _():
+                    at = (((core * N_FEAT + feat) * N_X + x) * N_Z + z) * first_count + k
+                    fetch(main, at, found).start()
+
+                @pl.when(k >= first_count)
+                def _():
+                    at = (((core * N_X + x) * N_FEAT + feat) * N_Z + z) * (
+                        depth - first_count
+                    ) + (k - first_count)
+                    fetch(side, at, found).start()
+
             found = found + (tag >= 0).astype(jnp.int32)
         return found
 
     total = lax.fori_loop(0, N_DOC, listed, 0)
-
-    def fetch(at, slot):
-        return (
-            pltpu.make_async_copy(
-                main.at[lists[1, at]], zbuf.at[slot, pl.ds(0, PART)], main_sems.at[slot]
-            ),
-            pltpu.make_async_copy(
-                side.at[lists[2, at]], zbuf.at[slot, pl.ds(PART, REST)], side_sems.at[slot]
-            ),
-        )
-
-    for first in range(DEPTH):
-
-        @pl.when(first < total)
-        def _():
-            for copy in fetch(first, first):
-                copy.start()
-
+    groups = (total + TOGETHER - 1) // TOGETHER
+
+    def fill(at, carry):
+        lists[0, at] = 0
+        lists[1, at] = 0
+        fetch(main, 0, at).start()
+        return carry
+
+    lax.fori_loop(total, groups * TOGETHER, fill, 0)
     out[...] = jnp.zeros_like(out)
 
-    def add(at, carry):
-        slot = lax.rem(at, DEPTH)
-        for copy in fetch(at, slot):
-            copy.wait()
-        source = lists[3, at]
-        start = pl.multiple_of((source & 1) * TILE, TILE)
-        tile = inbox[lax.shift_right_logical(source, jnp.int32(1)), pl.ds(start, TILE), :]
-        product = lax.dot_general(
-            tile, zbuf[slot], (((0,), (0,)), ((), ())), preferred_element_type=jnp.float32
-        )
-        place = pl.multiple_of(lists[0, at] * TILE, TILE)
-        out[pl.ds(place, TILE), :] += product
-
-        @pl.when(at + DEPTH < total)
-        def _():
-            for copy in fetch(at + DEPTH, slot):
-                copy.start()
-
+    def add(group, carry):
+        first = group * TOGETHER
+        pltpu.make_async_copy(
+            main.at[pl.ds(0, TOGETHER)], zbuf.at[pl.ds(first, TOGETHER)], sems.at[group]
+        ).wait()
+        products = []
+        for lane in range(TOGETHER):
+            at = first + lane
+            source = lists[1, at]
+            start = pl.multiple_of((source & 1) * TILE, TILE)
+            tile = inbox[lax.shift_right_logical(source, jnp.int32(1)), pl.ds(start, TILE), :]
+            product = lax.dot_general(
+                tile, zbuf[at], (((0,), (0,)), ((), ())), preferred_element_type=jnp.float32
+            )
+            products.append(jnp.where(at < total, product, 0.0))
+        for lane in range(TOGETHER):
+            place = pl.multiple_of(lists[0, first + lane] * TILE, TILE)
+            out[pl.ds(place, TILE), :] += products[lane]
         return carry
 
-    lax.fori_loop(0, total, add, 0)
+    lax.fori_loop(0, groups, add, 0)
 
 
 def final_stage(depth, notes, b_offsets, a_offsets, inbox, main, side):
@@ -600,10 +637,9 @@
         ],
         out_specs=pl.BlockSpec(memory_space=VMEM),
         scratch_shapes=[
-            pltpu.SMEM((4, 2 * N_DOC + 1), jnp.int32),
+            pltpu.SMEM((2, DEPTH), jnp.int32),
             pltpu.VMEM((DEPTH, TILE, SKETCH), jnp.bfloat16),
-            pltpu.SemaphoreType.DMA((DEPTH,)),
-            pltpu.SemaphoreType.DMA((DEPTH,)),
+            pltpu.SemaphoreType.DMA((DEPTH // TOGETHER,)),
         ],
     )(notes, b_offsets, a_offsets, inbox, main, side)
 
@@ -621,8 +657,18 @@
     a_offsets,
     omega_seed,
 ):
-    outbox = pack_stage(a_tags[:, 0], a_rows[:, 0], a_count[:, 0], a_tiles)
-    partial = text_stage(b_rows[:, 0], b_cols[:, 0], b_count[:, 0], omega_seed, b_offsets, b_tiles)
+    partial, outbox = text_stage(
+        b_rows[:, 0],
+        b_cols[:, 0],
+        b_count[:, 0],
+        omega_seed,
+        b_offsets,
+        a_tags[:, 0],
+        a_rows[:, 0],
+        a_count[:, 0],
+        b_tiles,
+        a_tiles,
+    )
 
     def rest(depth, partial, outbox):
         main, side, inbox = exchange_stage(depth, partial, outbox)

time: 228 us -> 203 us (0.89); the launches traced: 225 us -> 202 us
  Pallas kernels: 218 us -> 196 us
    pallas_call x1, Pallas kernels: 27.4 us -> 14.8 us  [final_stage(): pl.pallas_call(functools.partial(final_kernel, depth), out_shape=jax.Shap...]
    pallas_call x1, Pallas kernels: 167 us -> 160 us  [exchange_stage(): pl.pallas_call(functools.partial(exchange_kernel, depth), out_shape=(jax....]
    pallas_call x2 -> x1, Pallas kernels: 24.1 us -> 20.7 us  [text_stage(): pl.pallas_call(text_kernel, out_shape=(jax.ShapeDtypeStruct(rows_shape, j...]
where the time goes in v3:
time: 203 us; the launch traced here: 202 us
  Pallas kernels  196 us (97%)
  between operations  2.65 us (1%)
  local copies, waits for them, and re-layouts  2.23 us (1%)
    pallas_call x1, Pallas kernels, exchange_stage(): pl.pallas_call(functools.partial(exchange_kernel, depth), out_shape=(jax....  160 us
    pallas_call x1, Pallas kernels, text_stage(): pl.pallas_call(text_kernel, out_shape=(jax.ShapeDtypeStruct(rows_shape, j...  20.7 us
    pallas_call x1, Pallas kernels, final_stage(): pl.pallas_call(functools.partial(final_kernel, depth), out_shape=jax.Shap...  14.8 us

profile of v3, /device:TPU:24, one launch (start us, length us, event | category | flops | bytes accessed | tf_op | source)
XLA Modules:
  0.0 202.1 jit_solution(6554863628413181237)
XLA Ops:
  0.0 0.0 copy-start
  0.0 0.0 copy-start.1
  2.0 0.8 slice.13
  2.7 0.8 slice.12
  3.5 0.6 subtract_reduce_fusion
  4.8 20.7 %text.1 = (bf16[24,128,256]{2,1,0:T(8,128)(2,1)S(1)}, bf16[64,272,128]{2,1,0:T(8,128)(2,1)}) custom-call(s32[192]{0:T(256)} %bitcast.30, s32[192]{0:T(256)} %bitcast.31, s32[1]{0:T(128)} %bitcast.16.count, s32[1]{0:T(128)S(6)} %copy.18.seed, s32[65]{0:T(128)} %offsets.1, s32[64]{0:T(128)} %bitcast.32, s32[64]{0:T(128)} %bitcast.33, s32[1]{0:T(128)} %bitcast.17.tag_count, ...), custom_call_target="tpu_custom_call" | custom-call | flops 1700000000 | bytes 8000000 | tf_op jit(solution)/shard_map/text/pallas_call | solution.py:154
  25.5 0.0 copy-done
  25.5 0.0 copy-done.1
  25.5 176.6 %conditional.1 = (f32[4096,256]{1,0:T(8,128)}) conditional(s32[]{:T(128)} %convert_element_type.17, (bf16[24,128,256]{2,1,0:T(8,128)(2,1)S(1)}, bf16[64,272,128]{2,1,0:T(8,128)(2,1)}, s32[65]{0:T(128)S(1)}, s32[65]{0:T(128)S(1)}) %tuple.18, (bf16[24,128,256]{2,1,0:T(8,128)(2,1)S(1)}, bf16[64,272,128]{2,1,0:T(8,128)(2,1)}, s32[65]{0:T(128)S(1)}, ...), branch_computations={%region_1.0_spmd, %region_2.0_spmd} | conditional | flops 256 | bytes 3592 | solution.py:679
  25.5 160.1 %exchange_2.1 = (bf16[2,4,4,8,1,128,256]{6,5,4,3,2,1,0:T(8,128)(2,1)}, bf16[2,4,4,8,1,128,256]{6,5,4,3,2,1,0:T(8,128)(2,1)}, bf16[4,16,272,128]{3,2,1,0:T(8,128)(2,1)}, bf16[4,16,272,128]{3,2,1,0:T(8,128)(2,1)}) custom-call(bf16[3,2,4,128,256]{4,3,2,1,0:T(8,128)(2,1)S(1)} %bitcast.25, bf16[4,16,272,128]{3,2,1,0:T(8,128)(2,1)} %bitcast.20), custom_call_target="tpu_custom_call" | custom-call | tf_op jit(solution)/shard_map/cond/branch_1_fun/exchange_2/pallas_call | solution.py:502
  185.6 1.0 fusion.1
  186.7 0.7 reshape.39.notes
  187.3 14.8 %branch_1_fun.1 = f32[4096,256]{1,0:T(8,128)} custom-call(s32[256]{0:T(256)} %reshape.39.notes, s32[65]{0:T(128)S(1)} %get-tuple-element.34.b_offsets, s32[65]{0:T(128)S(1)} %get-tuple-element.35.a_offsets, bf16[64,272,128]{2,1,0:T(8,128)(2,1)} %bitcast.29, bf16[256,128,256]{2,1,0:T(8,128)(2,1)} %bitcast.22, bf16[256,128,256]{2,1,0:T(8,128)(2,1)} %bitcast.23), custom_call_target="tpu_custom_call" | custom-call | tf_op jit(solution)/shard_map/cond/branch_1_fun/pallas_call | solution.py:627
Async XLA Ops:
  0.0 25.5 %copy-start = (s32[65]{0:T(128)S(1)}, s32[65]{0:T(128)}, u32[]{:S(2)}) copy-start(s32[65]{0:T(128)} %offsets.1) | copy-start | bytes 784
  0.0 25.5 %copy-start.1 = (s32[65]{0:T(128)S(1)}, s32[65]{0:T(128)}, u32[]{:S(2)}) copy-start(s32[65]{0:T(128)} %param.22) | copy-start | bytes 784

commit v4 on v3

v4 whole, which is shorter than its diff:
```python
import functools

import jax
import jax.numpy as jnp
from jax import lax
from jax.experimental import pallas as pl
from jax.experimental.pallas import tpu as pltpu
from jax.sharding import PartitionSpec as P

TILE = 128
SKETCH = 256
TERMS = 2097152
TAG_DEV = 4096
ROWB_MAX = 12
OWNED = TAG_DEV // TILE
N_DOC = 64
N_FEAT = 4
META = 16
PAGE = 2 * TILE + META
CHUNK = 16
GROUP = 4
TOGETHER = 4
DEPTH = 2 * N_DOC
PAIR_MAX = 2 * ROWB_MAX
N_X = 4
N_Z = 8
N_CORE = 2
WIDE = N_Z * N_CORE
MESH = pl.DeviceIdType.MESH

VMEM = pltpu.MemorySpace.VMEM
SMEM = pltpu.MemorySpace.SMEM
ANY = pl.ANY


def shr(value, count):
    return lax.shift_right_logical(value, jnp.full(value.shape, count, jnp.int32))


def pack_kernel(tags, tag_rows, count, tiles, *refs):
    outs = refs[:N_X]
    meta, seen, notes, sems, meta_sems = refs[N_X:]
    used = count[0]
    x = lax.axis_index("doc") // WIDE

    def clear(owner, carry):
        seen[owner] = 0
        for lane in range(4):
            notes[owner * 4 + lane] = 0
        return carry

    lax.fori_loop(0, N_DOC, clear, 0)

    def put(at, step, lane, rank):
        start = pl.multiple_of(rank * TILE, TILE)
        return pltpu.make_async_copy(
            tiles.at[at], outs[step].at[lane, pl.ds(start, TILE), :], sems.at[at]
        )

    def send(at, carry):
        tag = tags[at]
        owner = lax.shift_right_logical(tag, jnp.int32(7))
        rank = jnp.minimum(seen[owner], 1)
        seen[owner] = rank + 1
        notes[owner * 4 + rank * 2] = (tag & (OWNED - 1)) + 1
        notes[owner * 4 + rank * 2 + 1] = tag_rows[at]
        away = (lax.shift_right_logical(owner, jnp.int32(4)) - x) & (N_X - 1)
        for step in range(N_X):

            @pl.when(away == step)
            def _():
                put(at, step, owner & (WIDE - 1), rank).start()

        return carry

    lax.fori_loop(0, used, send, 0)
    lane_iota = lax.broadcasted_iota(jnp.int32, (META, TILE), 1)

    def note(owner, carry):
        value = jnp.zeros((META, TILE), jnp.int32)
        for lane in range(4):
            value = jnp.where(lane_iota == lane, notes[owner * 4 + lane], value)
        meta[owner] = value.astype(jnp.float32).astype(jnp.bfloat16)
        return carry

    lax.fori_loop(0, N_DOC, note, 0)

    def put_meta(step):
        start = lax.rem(x + step, N_X) * WIDE
        return pltpu.make_async_copy(
            meta.at[pl.ds(start, WIDE)],
            outs[step].at[:, pl.ds(2 * TILE, META), :],
            meta_sems.at[step],
        )

    for step in range(N_X):
        put_meta(step).start()

    def drain(at, carry):
        put(at, 0, 0, 0).wait()
        return carry

    lax.fori_loop(0, used, drain, 0)
    for step in range(N_X):
        put_meta(step).wait()


def pack_stage(a_tags, a_rows, a_count, a_tiles):
    return pl.pallas_call(
        pack_kernel,
        out_shape=(jax.ShapeDtypeStruct((WIDE, PAGE, TILE), jnp.bfloat16),) * N_X,
        in_specs=[pl.BlockSpec(memory_space=SMEM)] * 3 + [pl.BlockSpec(memory_space=VMEM)],
        out_specs=(pl.BlockSpec(memory_space=ANY),) * N_X,
        scratch_shapes=[
            pltpu.VMEM((N_DOC, META, TILE), jnp.bfloat16),
            pltpu.SMEM((N_DOC,), jnp.int32),
            pltpu.SMEM((N_DOC * 4,), jnp.int32),
            pltpu.SemaphoreType.DMA((a_tiles.shape[0],)),
            pltpu.SemaphoreType.DMA((N_X,)),
        ],
        name="pack",
    )(a_tags, a_rows, a_count, a_tiles)


def text_kernel(rows, cols, count, seed, offsets, tiles, out, acc, base):
    step = pl.program_id(0)

    @pl.when(step == 0)
    def _():
        row_iota = lax.broadcasted_iota(jnp.int32, (TILE, SKETCH), 0)
        col_iota = lax.broadcasted_iota(jnp.int32, (TILE, SKETCH), 1)
        start = (row_iota * SKETCH + col_iota) ^ (seed[0] * 747796405)
        base[...] = start ^ shr(start, 16)
        acc[...] = jnp.zeros_like(acc)

    doc = lax.axis_index("doc")
    first = offsets[doc] - offsets[doc - lax.rem(doc, 2)]
    slab = lax.axis_index("feat") * (TERMS // (TILE * N_FEAT))
    used = count[0]

    def some(width, first_at, group, carry):
        products = []
        for lane in range(width):
            at = first_at + group * width + lane
            block = (cols[step * CHUNK + at] + slab) * (TILE * SKETCH)
            block = block ^ lax.shift_right_logical(block, jnp.int32(16))
            mixing = base[...] ^ block
            mixing = mixing * 2146121005
            mixing = mixing ^ shr(mixing, 15)
            mixing = mixing * -2073254261
            mixing = mixing ^ shr(mixing, 16)
            levels = (shr(mixing, 8) & 65535).astype(jnp.float32)
            panel = ((levels - 32767.5) * (3.4641016 / 65536.0)).astype(jnp.bfloat16)
            products.append(jnp.dot(tiles[at], panel, preferred_element_type=jnp.float32))
        for lane in range(width):
            at = step * CHUNK + first_at + group * width + lane
            acc[rows[at] + first] += products[lane]
        return carry

    left = jnp.clip(used - step * CHUNK, 0, CHUNK)
    whole = left // GROUP
    lax.fori_loop(0, whole, functools.partial(some, GROUP, 0), 0)
    lax.fori_loop(0, left - whole * GROUP, functools.partial(some, 1, whole * GROUP), 0)

    @pl.when(step == pl.num_programs(0) - 1)
    def _():
        out[...] = acc[...].astype(jnp.bfloat16)


def text_stage(b_rows, b_cols, b_count, omega_seed, b_offsets, b_tiles):
    rows_shape = (PAIR_MAX, TILE, SKETCH)
    return pl.pallas_call(
        text_kernel,
        out_shape=jax.ShapeDtypeStruct(rows_shape, jnp.bfloat16),
        grid=(b_tiles.shape[0] // CHUNK,),
        in_specs=[pl.BlockSpec(memory_space=SMEM)] * 5
        + [pl.BlockSpec((CHUNK, TILE, TILE), lambda i: (i, 0, 0))],
        out_specs=pl.BlockSpec(rows_shape, lambda i: (0, 0, 0)),
        scratch_shapes=[
            pltpu.VMEM(rows_shape, jnp.float32),
            pltpu.VMEM((TILE, SKETCH), jnp.int32),
        ],
        cost_estimate=pl.CostEstimate(
            flops=20000000000, bytes_accessed=40000000, transcendentals=0
        ),
        name="text",
    )(b_rows, b_cols, b_count, omega_seed, b_offsets, b_tiles)


def sum_kernel(
    partial, tiles, rows, near, own, core_in, sums, feat_in, core_sem, load_sem, feat_sem, near_sem
):
    depth = rows.shape[0]
    doc = lax.axis_index("doc")
    feat = lax.axis_index("feat")
    core = lax.rem(doc, N_CORE)
    sibling = (doc - core + (1 - core), feat)

    def other(step):
        return lax.rem(feat + step, N_FEAT)

    lane = lax.rem(doc, WIDE)

    def beside(step):
        return lax.rem(lane + step, WIDE)

    barrier = pltpu.get_barrier_semaphore()

    def greet(step, carry):
        pl.semaphore_signal(
            barrier, inc=1, device_id=(doc - lane + beside(step), feat), device_id_type=MESH
        )
        return carry

    lax.fori_loop(1, WIDE, greet, 0)
    for step in range(1, N_FEAT):
        pl.semaphore_signal(barrier, inc=1, device_id=(doc, other(step)), device_id_type=MESH)
    pl.semaphore_wait(barrier, WIDE - 1 + N_FEAT - 1)

    from_core = pltpu.make_async_remote_copy(
        src_ref=partial.at[:, 1 - core],
        dst_ref=core_in,
        send_sem=core_sem.at[0],
        recv_sem=core_sem.at[1],
        device_id=sibling,
        device_id_type=MESH,
    )
    from_core.start()
    load = pltpu.make_async_copy(partial.at[:, core], own, load_sem)
    load.start()

    def tiles_to(step):
        return pltpu.make_async_remote_copy(
            src_ref=tiles.at[beside(step)],
            dst_ref=near.at[lane],
            send_sem=near_sem.at[0, step],
            recv_sem=near_sem.at[1, step],
            device_id=(doc - lane + beside(step), feat),
            device_id_type=MESH,
        )

    def send_tiles(step, carry):
        tiles_to(step).start()
        return carry

    lax.fori_loop(1, WIDE, send_tiles, 0)
    keep = pltpu.make_async_copy(tiles.at[lane], near.at[lane], near_sem.at[0, 0])
    keep.start()
    load.wait()
    from_core.wait()

    def to_feat(step):
        return pltpu.make_async_remote_copy(
            src_ref=sums.at[other(step)],
            dst_ref=feat_in.at[step - 1],
            send_sem=feat_sem.at[0, step],
            recv_sem=feat_sem.at[1, step],
            device_id=(doc, other(step)),
            device_id_type=MESH,
        )

    for step in (2, 1, 3, 0):
        to = other(step)
        for k in range(depth):
            sums[to, k] = own[k, to] + core_in[k, to]
        if step:
            to_feat(step).start()
    for step in (1, 3, 2):
        to_feat(step).wait_recv()
    for k in range(depth):
        terms = [
            block[k].astype(jnp.float32)
            for block in (sums.at[feat], feat_in.at[0], feat_in.at[1], feat_in.at[2])
        ]
        rows[k] = ((terms[0] + terms[1]) + (terms[2] + terms[3])).astype(jnp.bfloat16)
    for step in (1, 2, 3):
        to_feat(step).wait_send()

    def settle(step, carry):
        tiles_to(step).wait_recv()
        tiles_to(step).wait_send()
        return carry

    lax.fori_loop(1, WIDE, settle, 0)
    keep.wait()


def sum_stage(partial, tiles):
    bf16 = jnp.bfloat16
    dma = pltpu.SemaphoreType.DMA
    depth = PAIR_MAX // 8
    block = (TILE, SKETCH)
    return pl.pallas_call(
        sum_kernel,
        out_shape=(
            jax.ShapeDtypeStruct((depth,) + block, bf16),
            jax.ShapeDtypeStruct((WIDE, PAGE, TILE), bf16),
        ),
        in_specs=[pl.BlockSpec(memory_space=ANY)] * 2,
        out_specs=(pl.BlockSpec(memory_space=VMEM), pl.BlockSpec(memory_space=ANY)),
        scratch_shapes=[
            pltpu.VMEM((depth, N_FEAT) + block, bf16),
            pltpu.VMEM((depth, N_FEAT) + block, bf16),
            pltpu.VMEM((N_FEAT, depth) + block, bf16),
            pltpu.VMEM((N_FEAT - 1, depth) + block, bf16),
            dma((2,)),
            dma,
            dma((2, 4)),
            dma((2, WIDE)),
        ],
        compiler_params=pltpu.CompilerParams(collective_id=1, has_side_effects=True),
        cost_estimate=pl.CostEstimate(
            flops=20000000000, bytes_accessed=40000000, transcendentals=0
        ),
        name="sum",
    )(partial.reshape(depth, N_CORE, N_FEAT, TILE, SKETCH), tiles)


def exchange_kernel(
    depth,
    rows,
    tiles_1,
    tiles_2,
    tiles_3,
    main,
    side,
    inbox,
    place_sem,
    z_sem,
    second_sem,
    third_sem,
    pair_sem,
    tiles_sem,
    keep_sem,
):
    count = main.shape[4]
    main_own = rows.at[pl.ds(0, count)]
    side_own = rows.at[pl.ds(count, depth - count)]
    doc = lax.axis_index("doc")
    feat = lax.axis_index("feat")
    core = lax.rem(doc, N_CORE)
    z = lax.rem(doc // N_CORE, N_Z)
    x = doc // (N_CORE * N_Z)
    lane = z * N_CORE + core

    def device(x_to, z_to, core_to, feat_to):
        return ((x_to * N_Z + z_to) * N_CORE + core_to, feat_to)

    def turn(value, step, size):
        return lax.rem(value + (step % size), size)

    sibling = device(x, z, 1 - core, feat)

    def remote(source, target, sems, to):
        return pltpu.make_async_remote_copy(
            src_ref=source,
            dst_ref=target,
            send_sem=sems[0],
            recv_sem=sems[1],
            device_id=to,
            device_id_type=MESH,
        )

    barrier = pltpu.get_barrier_semaphore()

    def greet(step, carry):
        other = lax.rem(lane + step, N_Z * N_CORE)
        pl.semaphore_signal(
            barrier, inc=1, device_id=(x * (N_Z * N_CORE) + other, feat), device_id_type=MESH
        )
        return carry

    lax.fori_loop(1, N_Z * N_CORE, greet, 0)
    for step in (1, 3):
        pl.semaphore_signal(
            barrier, inc=1, device_id=device(turn(x, step, N_X), z, core, feat), device_id_type=MESH
        )
    for step in (1, 3):
        pl.semaphore_signal(
            barrier, inc=1, device_id=device(x, z, core, turn(feat, step, N_FEAT)), device_id_type=MESH
        )
    pl.semaphore_wait(barrier, N_Z * N_CORE - 1 + 4)

    place_main = pltpu.make_async_copy(main_own, main.at[core, feat, x, z], place_sem.at[0])
    place_side = pltpu.make_async_copy(side_own, side.at[core, x, feat, z], place_sem.at[1])
    place_main.start()
    place_side.start()

    upper = TILE // 2

    def ring_z(way, which, step):
        sign = 1 if way == 0 else -1
        block = turn(z, -sign * (step - 1), N_Z)
        held = main.at[core, feat, x, block] if which == 0 else side.at[core, x, feat, block]
        source = held if step > 1 else (main_own if which == 0 else side_own)
        if step == N_Z // 2:
            part = pl.ds(way * upper, upper)
            held = held.at[:, part]
            source = source.at[:, part]
        return remote(
            source, held, (z_sem.at[0, way, which, step], z_sem.at[1, way, which, step]),
            device(x, turn(z, sign, N_Z), core, feat),
        )

    def spread(block, mine):
        half = N_Z // 2
        for sems, at, axis, which in (
            (second_sem, 1, 1, 1),
            (second_sem, 0, 0, 0),
            (third_sem, 0, 1, 0),
            (third_sem, 4, 0, 1),
        ):
            held = (main.at[core, feat, x] if which == 0 else side.at[core, x, feat]).at[block]
            source = held
            if mine:
                source = main_own if which == 0 else side_own
            for way in range(2):
                sign = 1 if way == 0 else -1
                if axis == 0:
                    to = device(turn(x, sign, N_X), z, core, feat)
                else:
                    to = device(x, z, core, turn(feat, sign, N_FEAT))
                part = block // half
                number = way * 3 + (part if way == 0 else 1 - part)
                remote(source, held, (sems.at[0, at, number], sems.at[1, at, number]), to).start()

    for step in range(1, N_Z // 2 + 1):
        for way in range(2):
            for which in range(2):
                if step > 1:
                    ring_z(way, which, step - 1).wait_recv()
                ring_z(way, which, step).start()
        if step == 1:
            spread(z, True)
        else:
            spread(turn(z, 1 - step, N_Z), False)
            spread(turn(z, step - 1, N_Z), False)
    for way in range(2):
        for which in range(2):
            ring_z(way, which, N_Z // 2).wait_recv()
    spread(turn(z, N_Z // 2, N_Z), False)
    place_main.wait()
    place_side.wait()

    half = N_Z // 2

    def ring_four(sems, at, axis, block, kind):
        way, part, hop = kind
        sign = 1 if way == 0 else -1
        if axis == 0:
            place, to = x, device(turn(x, sign, N_X), z, core, feat)
        else:
            place, to = feat, device(x, z, core, turn(feat, sign, N_FEAT))
        ref = block(turn(place, -sign * (hop - 1), 4)).at[pl.ds(part * half, half)]
        number = way * 3 + (part ^ way if hop == 1 else 2)
        return remote(ref, ref, (sems.at[0, at, number], sems.at[1, at, number]), to)

    first_kinds = ((0, 0, 1), (1, 1, 1), (0, 1, 1), (1, 0, 1))
    later_kinds = ((0, 0, 2), (1, 1, 2))

    def main_block(feat_at, x_at):
        return main.at[core, feat_at, x_at]

    def side_block(x_at, feat_at):
        return side.at[core, x_at, feat_at]

    def second(which, kind):
        if which == 0:
            return ring_four(second_sem, 0, 0, lambda i: main_block(feat, i), kind)
        return ring_four(second_sem, 1, 1, lambda i: side_block(x, i), kind)

    def third(which, step, kind):
        if which == 0:
            chunk = turn(x, step, N_X)
            return ring_four(third_sem, step, 1, lambda i: main_block(i, chunk), kind)
        chunk = turn(feat, step, N_FEAT)
        return ring_four(third_sem, 4 + step, 0, lambda i: side_block(i, chunk), kind)

    def to_sibling(which, far, step):
        if which == 0:
            ref = main_block(turn(feat, far, N_FEAT), turn(x, step, N_X))
        else:
            ref = side_block(turn(x, far, N_X), turn(feat, step, N_FEAT))
        at = which * 16 + far * 4 + step
        return remote(ref, ref, (pair_sem.at[0, at], pair_sem.at[1, at]), sibling)

    to_sibling(0, 0, 0).start()
    to_sibling(1, 0, 0).start()

    def tiles_to(step, source, from_x):
        other = lax.rem(lane + step, N_Z * N_CORE)
        return remote(
            source.at[other], inbox.at[from_x, lane],
            (tiles_sem.at[0, from_x, step], tiles_sem.at[1, from_x, step]),
            (x * (N_Z * N_CORE) + other, feat),
        )

    def send_tiles(source, from_x, at):
        def one(step, carry):
            tiles_to(step, source, from_x).start()
            return carry

        lax.fori_loop(1, N_Z * N_CORE, one, 0)
        pltpu.make_async_copy(source.at[lane], inbox.at[from_x, lane], keep_sem.at[at]).start()

    for step, source in enumerate((tiles_1, tiles_2, tiles_3)):
        send_tiles(source, step, step)

    def pass_on_second(which):
        for kind in later_kinds:
            way, part, _ = kind
            second(which, (way, part, 1)).wait_recv()
            second(which, kind).start()

    def finish_second(which):
        second(which, (0, 1, 1)).wait_recv()
        for kind in first_kinds:
            third(which, 3, kind).start()
        to_sibling(which, 0, 3).start()
        second(which, (1, 0, 1)).wait_recv()
        for kind in first_kinds:
            third(which, 1, kind).start()
        to_sibling(which, 0, 1).start()

    def finish_far(which):
        for kind in later_kinds:
            second(which, kind).wait_recv()
        for kind in first_kinds:
            third(which, 2, kind).start()
        to_sibling(which, 0, 2).start()

    def pass_on_third(which, step):
        for kind in later_kinds:
            way, part, _ = kind
            third(which, step, (way, part, 1)).wait_recv()
            third(which, step, kind).start()

    def finish_third(which, step):
        third(which, step, (0, 1, 1)).wait_recv()
        to_sibling(which, 3, step).start()
        third(which, step, (1, 0, 1)).wait_recv()
        to_sibling(which, 1, step).start()
        for kind in later_kinds:
            third(which, step, kind).wait_recv()
        to_sibling(which, 2, step).start()

    pass_on_second(1)
    pass_on_second(0)
    finish_second(1)
    finish_second(0)
    pass_on_third(1, 0)
    pass_on_third(0, 0)
    finish_far(1)
    finish_far(0)
    finish_third(1, 0)
    finish_third(0, 0)
    for step in (3, 1, 2):
        pass_on_third(1, step)
        pass_on_third(0, step)
        finish_third(1, step)
        finish_third(0, step)

    for which in range(2):
        for far in range(4):
            for step in range(4):
                to_sibling(which, far, step).wait_recv()
                to_sibling(which, far, step).wait_send()
        for kind in first_kinds + later_kinds:
            second(which, kind).wait_send()
        for step in range(4):
            for kind in first_kinds + later_kinds:
                third(which, step, kind).wait_send()
        for way in range(2):
            for step in range(1, N_Z // 2 + 1):
                ring_z(way, which, step).wait_send()
    def settle(from_x, carry):
        def one(step, inner):
            copy = tiles_to(step, tiles_1, from_x)
            copy.wait_recv()
            copy.wait_send()
            return inner

        lax.fori_loop(1, N_Z * N_CORE, one, 0)
        pltpu.make_async_copy(tiles_1.at[0], inbox.at[0, 0], keep_sem.at[from_x]).wait()
        return carry

    lax.fori_loop(0, N_X - 1, settle, 0)


def exchange_stage(depth, rows, tiles):
    bf16 = jnp.bfloat16
    dma = pltpu.SemaphoreType.DMA
    block = (TILE, SKETCH)
    first = (depth + 1) // 2
    main, side, inbox = pl.pallas_call(
        functools.partial(exchange_kernel, depth),
        out_shape=(
            jax.ShapeDtypeStruct((N_CORE, N_FEAT, N_X, N_Z, first) + block, bf16),
            jax.ShapeDtypeStruct((N_CORE, N_X, N_FEAT, N_Z, depth - first) + block, bf16),
            jax.ShapeDtypeStruct((N_X - 1, WIDE, PAGE, TILE), bf16),
        ),
        in_specs=[pl.BlockSpec(memory_space=VMEM)] + [pl.BlockSpec(memory_space=ANY)] * (N_X - 1),
        out_specs=(pl.BlockSpec(memory_space=ANY),) * 3,
        scratch_shapes=[
            dma((2,)),
            dma((2, 2, 2, N_Z // 2 + 1)),
            dma((2, 2, 6)),
            dma((2, 8, 6)),
            dma((2, 32)),
            dma((2, N_X - 1, WIDE)),
            dma((N_X - 1,)),
        ],
        compiler_params=pltpu.CompilerParams(collective_id=depth, has_side_effects=True),
        name="exchange_%d" % depth,
    )(rows, *tiles)
    return (
        main.reshape((-1,) + block),
        side.reshape((-1,) + block),
        inbox.reshape(N_DOC - WIDE, PAGE, TILE),
    )


def final_kernel(
    depth, notes, b_offsets, a_offsets, near, far, main, side,
    out, inbox, lists, zbuf, sems, tile_sems,
):
    first_count = (depth + 1) // 2
    loads = (
        pltpu.make_async_copy(near, inbox.at[pl.ds(0, WIDE)], tile_sems.at[0]),
        pltpu.make_async_copy(far, inbox.at[pl.ds(WIDE, N_DOC - WIDE)], tile_sems.at[1]),
    )
    for load in loads:
        load.start()
    here = lax.axis_index("doc") // WIDE

    def fetch(ref, at, slot):
        group = lax.shift_right_logical(slot, jnp.int32(2))
        return pltpu.make_async_copy(ref.at[at], zbuf.at[slot], sems.at[group])

    def listed(number, found):
        way = lax.shift_right_logical(number, jnp.int32(4))
        step = way + jnp.where(way == 2, 1, 0) - jnp.where(way == 3, 1, 0)
        doc = ((here - step) & (N_X - 1)) * WIDE + (number & (WIDE - 1))
        shift = a_offsets[doc]
        split = b_offsets[doc]
        before = jnp.maximum(doc - 1, 0)
        chips = [lax.shift_right_logical(at, jnp.int32(1)) for at in (before, doc)]
        bases = [shift - b_offsets[chip * 2] for chip in chips]
        for rank in range(2):
            tag = notes[number * 4 + rank * 2] - 1

            @pl.when(tag >= 0)
            def _():
                row = notes[number * 4 + rank * 2 + 1]
                early = row + shift < split
                chip = jnp.where(early, chips[0], chips[1])
                inner = jnp.clip(row + jnp.where(early, bases[0], bases[1]), 0, depth * 8 - 1)
                k = lax.shift_right_logical(inner, jnp.int32(3))
                core = lax.shift_right_logical(inner, jnp.int32(2)) & 1
                feat = inner & 3
                x = lax.shift_right_logical(chip, jnp.int32(3))
                z = chip & 7
                lists[0, found] = tag
                lists[1, found] = number * 2 + rank

                @pl.when(k < first_count)
                def _():
                    at = (((core * N_FEAT + feat) * N_X + x) * N_Z + z) * first_count + k
                    fetch(main, at, found).start()

                @pl.when(k >= first_count)
                def _():
                    at = (((core * N_X + x) * N_FEAT + feat) * N_Z + z) * (
                        depth - first_count
                    ) + (k - first_count)
                    fetch(side, at, found).start()

            found = found + (tag >= 0).astype(jnp.int32)
        return found

    total = lax.fori_loop(0, N_DOC, listed, 0)
    groups = (total + TOGETHER - 1) // TOGETHER

    def fill(at, carry):
        lists[0, at] = 0
        lists[1, at] = 0
        fetch(main, 0, at).start()
        return carry

    lax.fori_loop(total, groups * TOGETHER, fill, 0)
    out[...] = jnp.zeros_like(out)
    for load in loads:
        load.wait()

    def add(group, carry):
        first = group * TOGETHER
        pltpu.make_async_copy(
            main.at[pl.ds(0, TOGETHER)], zbuf.at[pl.ds(first, TOGETHER)], sems.at[group]
        ).wait()
        products = []
        for lane in range(TOGETHER):
            at = first + lane
            source = lists[1, at]
            start = pl.multiple_of((source & 1) * TILE, TILE)
            tile = inbox[lax.shift_right_logical(source, jnp.int32(1)), pl.ds(start, TILE), :]
            product = lax.dot_general(
                tile, zbuf[at], (((0,), (0,)), ((), ())), preferred_element_type=jnp.float32
            )
            products.append(jnp.where(at < total, product, 0.0))
        for lane in range(TOGETHER):
            place = pl.multiple_of(lists[0, first + lane] * TILE, TILE)
            out[pl.ds(place, TILE), :] += products[lane]
        return carry

    lax.fori_loop(0, groups, add, 0)


def final_stage(depth, notes, b_offsets, a_offsets, near, far, main, side):
    return pl.pallas_call(
        functools.partial(final_kernel, depth),
        out_shape=jax.ShapeDtypeStruct((TAG_DEV, SKETCH), jnp.float32),
        in_specs=[
            pl.BlockSpec(memory_space=SMEM),
            pl.BlockSpec(memory_space=SMEM),
            pl.BlockSpec(memory_space=SMEM),
            pl.BlockSpec(memory_space=ANY),
            pl.BlockSpec(memory_space=ANY),
            pl.BlockSpec(memory_space=ANY),
            pl.BlockSpec(memory_space=ANY),
        ],
        out_specs=pl.BlockSpec(memory_space=VMEM),
        scratch_shapes=[
            pltpu.VMEM((N_DOC, PAGE, TILE), jnp.bfloat16),
            pltpu.SMEM((2, DEPTH), jnp.int32),
            pltpu.VMEM((DEPTH, TILE, SKETCH), jnp.bfloat16),
            pltpu.SemaphoreType.DMA((DEPTH // TOGETHER,)),
            pltpu.SemaphoreType.DMA((2,)),
        ],
    )(notes, b_offsets, a_offsets, near, far, main, side)


def local(
    b_tiles,
    b_rows,
    b_cols,
    b_count,
    b_offsets,
    a_tiles,
    a_rows,
    a_tags,
    a_count,
    a_offsets,
    omega_seed,
):
    tiles = pack_stage(a_tags[:, 0], a_rows[:, 0], a_count[:, 0], a_tiles)
    moved = []
    for step in (1, 3, 2):
        route = [(at, (at + step * WIDE) % N_DOC) for at in range(N_DOC)]
        moved.append(lax.ppermute(tiles[step], "doc", route))
    partial = text_stage(
        b_rows[:, 0], b_cols[:, 0], b_count[:, 0], omega_seed, b_offsets, b_tiles
    )
    mine, near = sum_stage(partial, tiles[0])

    def rest(depth, rows, near, *tiles):
        main, side, far = exchange_stage(depth, rows, tiles)
        notes = jnp.concatenate([near[:, 2 * TILE, 0:4], far[:, 2 * TILE, 0:4]])
        notes = notes.astype(jnp.int32).reshape(-1)
        return final_stage(depth, notes, b_offsets, a_offsets, near, far, main, side)

    most = jnp.max(b_offsets[2::2] - b_offsets[:-1:2])
    return lax.cond(
        most <= 16, functools.partial(rest, 2), functools.partial(rest, 3), mine, near, *moved
    )


def solution(mesh):
    return jax.shard_map(
        local,
        mesh=mesh,
        in_specs=(
            P("doc", "feat", None),
            P("doc", "feat"),
            P("doc", "feat"),
            P("doc", "feat"),
            P(),
            P("doc", "feat", None),
            P("doc", "feat"),
            P("doc", "feat"),
            P("doc", "feat"),
            P(),
            P(),
        ),
        out_specs=P(("doc", "feat"), None),
        check_vma=False,
    )
```

time: 203 us -> 190 us (0.936)
  Pallas kernels: 196 us -> 176 us
  starting transfers between devices: 0 us -> 4.81 us
    pallas_call x1, Pallas kernels: 160 us -> 104 us  [exchange_stage(): pl.pallas_call(functools.partial(exchange_kernel, depth), out_shape=(jax....]
    pallas_call x1 -> x3, Pallas kernels: 20.7 us -> 58.9 us  [the longest x1 32.7 us: sum_stage(): pl.pallas_call(sum_kernel, out_shape=(jax.ShapeDtypeStruct((depth,) + blo...]
    ppermute x0 -> x3, starting transfers between devices: none -> 4.81 us  [local(): moved.append(lax.ppermute(tiles[step], 'doc', route))]
  transfers between devices with their start and end apart: 0 -> 3, of which waited for: 0 -> 0; matrix products, arithmetic and copies ran while one was open for 0% -> 1% of each run, Pallas kernels for 0% -> 29%
where the time goes in v4:
time: 190 us; the launch traced here: 188 us
  Pallas kernels  176 us (93%)
  starting transfers between devices  4.81 us (3%)
  local copies, waits for them, and re-layouts  3.45 us (2%)
  between operations  2.66 us (1%)
    pallas_call x1, Pallas kernels, exchange_stage(): pl.pallas_call(functools.partial(exchange_kernel, depth), out_shape=(jax....  104 us
    pallas_call x1, Pallas kernels, sum_stage(): pl.pallas_call(sum_kernel, out_shape=(jax.ShapeDtypeStruct((depth,) + blo...  32.7 us
    pallas_call x1, Pallas kernels, text_stage(): pl.pallas_call(text_kernel, out_shape=jax.ShapeDtypeStruct(rows_shape, jn...  20.8 us
    pallas_call x1, Pallas kernels, final_stage(): pl.pallas_call(functools.partial(final_kernel, depth), out_shape=jax.Shap...  13.1 us
    pallas_call x1, Pallas kernels, pack_stage(): pl.pallas_call(pack_kernel, out_shape=(jax.ShapeDtypeStruct((WIDE, PAGE,...  5.4 us
    ppermute x3, starting transfers between devices, local(): moved.append(lax.ppermute(tiles[step], 'doc', route))  4.81 us
  transfers between devices with their start and end apart: 3, of which 0 were waited for; matrix products, arithmetic and copies ran while one was open for 1% of the time, Pallas kernels for 29%

profile of v4, /device:TPU:24, one launch (start us, length us, event | category | flops | bytes accessed | tf_op | source)
XLA Modules:
  0.0 187.5 jit_solution(9309797260742370211)
XLA Ops:
  0.7 5.4 %pack.1 = (bf16[16,272,128]{2,1,0:T(8,128)(2,1)}, bf16[16,272,128]{2,1,0:T(8,128)(2,1)}, bf16[16,272,128]{2,1,0:T(8,128)(2,1)}, bf16[16,272,128]{2,1,0:T(8,128)(2,1)}) custom-call(s32[64]{0:T(128)} %bitcast.31, s32[64]{0:T(128)} %bitcast.32, s32[1]{0:T(128)} %bitcast.18.count, bf16[64,128,128]{2,1,0:T(8,128)(2,1)} %tiles.3), custom_call_target="tpu_custom_call" | custom-call | tf_op jit(solution)/shard_map/pack/pallas_call | solution.py:109
  6.1 1.3 collective-permute-start
  7.4 2.0 %collective-permute-start.1 = (bf16[16,272,128]{2,1,0:T(8,128)(2,1)}, bf16[16,272,128]{2,1,0:T(8,128)(2,1)S(1)}, u32[]{:S(2)}, u32[]{:S(2)}) collective-permute-start(bf16[16,272,128]{2,1,0:T(8,128)(2,1)} %get-tuple-element.66), channel_id=1, source_target_pairs={{0,192},{4,196},{8,200},{12,204},{16,208},{20,212},{24,216},{28,22... | collective-permute-start | bytes 3342344 | tf_op jit(solution)/shard_map/ppermute | solution.py:759
  9.4 1.5 collective-permute-start.2
  10.9 0.8 slice.19
  11.6 0.8 slice.18
  13.7 0.6 subtract_reduce_fusion
  15.0 20.8 %text.1 = bf16[24,128,256]{2,1,0:T(8,128)(2,1)} custom-call(s32[192]{0:T(256)} %bitcast.33, s32[192]{0:T(256)} %bitcast.34, s32[1]{0:T(128)} %bitcast.17.count, s32[1]{0:T(128)S(6)} %copy.30.seed, s32[65]{0:T(128)} %offsets.1, bf16[192,128,128]{2,1,0:T(8,128)(2,1)} %tiles.2), custom_call_target="tpu_custom_call" | custom-call | flops 20000000000 | bytes 40000000 | tf_op jit(solution)/shard_map/text/pallas_call | solution.py:172
  35.8 0.0 copy-start
  35.8 32.7 %sum.1 = (bf16[3,128,256]{2,1,0:T(8,128)(2,1)S(1)}, bf16[16,272,128]{2,1,0:T(8,128)(2,1)S(1)}) custom-call(bf16[3,2,4,128,256]{4,3,2,1,0:T(8,128)(2,1)} %bitcast.35, bf16[16,272,128]{2,1,0:T(8,128)(2,1)} %get-tuple-element.62.tiles), custom_call_target="tpu_custom_call" | custom-call | flops 20000000000 | bytes 40000000 | tf_op jit(solution)/shard_map/sum/pallas_call | solution.py:293
  68.5 0.0 collective-permute-done
  68.5 0.0 collective-permute-done.1
  68.5 0.0 collective-permute-done.2
  68.5 0.0 copy-done
  68.5 119.0 %conditional.1 = (f32[4096,256]{1,0:T(8,128)}) conditional(s32[]{:T(128)} %convert_element_type.17, (bf16[16,272,128]{2,1,0:T(8,128)(2,1)S(1)}, bf16[3,128,256]{2,1,0:T(8,128)(2,1)S(1)}, bf16[16,272,128]{2,1,0:T(8,128)(2,1)S(1)}, bf16[16,272,128]{2,1,0:T(8,128)(2,1)S(1)}, bf16[16,272,128]{2,1,0:T(8,128)(2,1)}, /*index=5*/s32[65]{0:T(128)S(1)}, ...), branch_computations={%region_1.0_spmd, %region_2.0_spmd} | conditional | flops 1024 | bytes 8756 | solution.py:772
  68.5 0.1 copy.23
  68.6 103.9 %exchange_2.1 = (bf16[2,4,4,8,1,128,256]{6,5,4,3,2,1,0:T(8,128)(2,1)}, bf16[2,4,4,8,1,128,256]{6,5,4,3,2,1,0:T(8,128)(2,1)}, bf16[3,16,272,128]{3,2,1,0:T(8,128)(2,1)}) custom-call(bf16[3,128,256]{2,1,0:T(8,128)(2,1)S(1)} %get-tuple-element.47.rows, bf16[16,272,128]{2,1,0:T(8,128)(2,1)S(1)} %get-tuple-element.48.tiles_1, ...), custom_call_target="tpu_custom_call" | custom-call | tf_op jit(solution)/shard_map/cond/branch_1_fun/exchange_2/pallas_call | solution.py:595
  172.5 0.9 slice.21
  173.4 0.1 copy.24
  173.5 0.1 maximum_convert_fusion.1
  173.6 0.1 copy.25
  173.7 0.7 reshape.31.notes
  174.4 0.0 copy-done.2
  174.4 13.1 %branch_1_fun.1 = f32[4096,256]{1,0:T(8,128)} custom-call(s32[256]{0:T(256)} %reshape.31.notes, s32[65]{0:T(128)S(1)} %get-tuple-element.52.b_offsets, s32[65]{0:T(128)S(1)} %copy-done.2, bf16[16,272,128]{2,1,0:T(8,128)(2,1)S(1)} %get-tuple-element.46.near, bf16[48,272,128]{2,1,0:T(8,128)(2,1)} %bitcast.26, bf16[256,128,256]{2,1,0:T(8,128)(2,1)} %bitcast.21, ...), custom_call_target="tpu_custom_call" | custom-call | tf_op jit(solution)/shard_map/cond/branch_1_fun/pallas_call | solution.py:719
  (2 shorter events, 0.0 us)
Async XLA Ops:
  6.1 62.4 %collective-permute-start = (bf16[16,272,128]{2,1,0:T(8,128)(2,1)}, bf16[16,272,128]{2,1,0:T(8,128)(2,1)S(1)}, u32[]{:S(2)}, u32[]{:S(2)}) collective-permute-start(bf16[16,272,128]{2,1,0:T(8,128)(2,1)} %get-tuple-element.65), channel_id=1, source_target_pairs={{0,64},{4,68},{8,72},{12,76},{16,80},{20,84},{24,88},{28,92},{32,9... | collective-permute-start | bytes 3342344 | tf_op jit(solution)/shard_map/ppermute | solution.py:759
  7.4 61.1 %collective-permute-start.1 = (bf16[16,272,128]{2,1,0:T(8,128)(2,1)}, bf16[16,272,128]{2,1,0:T(8,128)(2,1)S(1)}, u32[]{:S(2)}, u32[]{:S(2)}) collective-permute-start(bf16[16,272,128]{2,1,0:T(8,128)(2,1)} %get-tuple-element.66), channel_id=1, source_target_pairs={{0,192},{4,196},{8,200},{12,204},{16,208},{20,212},{24,216},{28,22... | collective-permute-start | bytes 3342344 | tf_op jit(solution)/shard_map/ppermute | solution.py:759
  9.4 59.1 %collective-permute-start.2 = (bf16[16,272,128]{2,1,0:T(8,128)(2,1)}, bf16[16,272,128]{2,1,0:T(8,128)(2,1)}, u32[]{:S(2)}, u32[]{:S(2)}) collective-permute-start(bf16[16,272,128]{2,1,0:T(8,128)(2,1)} %get-tuple-element.67), channel_id=1, source_target_pairs={{0,128},{4,132},{8,136},{12,140},{16,144},{20,148},{24,152},{28,15... | collective-permute-start | bytes 3342344 | tf_op jit(solution)/shard_map/ppermute | solution.py:759
  35.8 32.7 %copy-start = (s32[65]{0:T(128)S(1)}, s32[65]{0:T(128)}, u32[]{:S(2)}) copy-start(s32[65]{0:T(128)} %offsets.1) | copy-start | bytes 784
  68.6 105.8 %copy-start.2 = (s32[65]{0:T(128)S(1)}, s32[65]{0:T(128)}, u32[]{:S(2)}) copy-start(s32[65]{0:T(128)} %get-tuple-element.72.a_offsets) | copy-start | bytes 784 | tf_op jit(solution)/shard_map/cond
